TPU v7x, 256 devices: a whole 4x4x8 slice. The times are simulated.
256 devices in a mesh: ctx: 32 (over z, y_lo, core), head: 8 (over x, y_hi).
Axes of the slice: x: 4, y: 4 (y_hi: 2, y_lo: 2; y = y_hi * 2 + y_lo), z: 8, core: 2. Of those that a mesh axis runs over, the one named last changes fastest.
Arguments:
- patch_hidden: bfloat16 [2048, 4096], P('ctx', 'head'), may hold values from -6 to 6
- queries: bfloat16 [2048, 32, 128], P('ctx', 'head'), may hold values from -6 to 6
- new_keys: bfloat16 [2048, 32, 128], P('ctx', 'head'), may hold values from -6 to 6
- new_values: bfloat16 [2048, 32, 128], P('ctx', 'head'), may hold values from -6 to 6
- cache_keys: bfloat16 [32768, 32, 128], P('ctx', 'head'), may hold values from -6 to 6
- cache_values: bfloat16 [32768, 32, 128], P('ctx', 'head'), may hold values from -6 to 6
- cache_request: int32 [32768], P('ctx'), may hold values from 0 to 7, never falling along the last dimension, each value on 1 to 8192 neighbouring positions
- new_request: int32 [2048], replicated, may hold values from 0 to 7, as said below
- out_weight: bfloat16 [32, 128, 4096], P('head'), may hold values from -0.375 to 0.375
- norm_gain: float32 [4096], replicated, may hold values from 0.1 to 1.9
- dec_kv_weight: bfloat16 [4096, 2, 1024], P(None, None, 'head'), may hold values from -0.09375 to 0.09375
- dec_query_weight: bfloat16 [1024, 1024], P(None, 'head'), may hold values from -0.1875 to 0.1875
- query_gain: float32 [64], replicated, may hold values from 0.1 to 1.9
- key_gain: float32 [64], replicated, may hold values from 0.1 to 1.9
- dec_out_weight: bfloat16 [1024, 1024], P('head'), may hold values from -0.75 to 0.75
- byte_states: bfloat16 [8192, 1024], P('ctx'), may hold values from -6 to 6
- byte_patch: int32 [8192], P('ctx'), may hold values from 0 to 2047, never falling along the last dimension, each value on 1 to 8 neighbouring positions
Outputs:
- patch_out: bfloat16 [2048, 4096], P('ctx', 'head')
- byte_out: bfloat16 [8192, 1024], P('ctx', 'head')
Inputs may be any that keep to these rules, and one draw needn't show every extreme that they name: `new_request`: never falls along the patches; every request of 0 to 7 has an even number, two or more, of new patches. `cache_request`: never falls along the cached patches; every request has one or more cached patches. `byte_patch`: never falls along the bytes; every new patch owns one or more bytes.
All inputs are finite; a program needn't handle non-finite values.
Results may differ from a plain program's by a relative error of at most 0.017.
Values may be sent and summed in bfloat16 or wider, within the bound.
A program may use at most 128 MiB of HBM per device.

v0:
```python
import jax
import jax.numpy as jnp
from jax import lax
from jax.sharding import PartitionSpec as P

DEC_DH = 64


def joined_along(pieces, dim):
    shape = list(pieces.shape[1:])
    shape[dim] *= pieces.shape[0]
    return jnp.moveaxis(pieces, 0, dim).reshape(shape)


def sent_to_all(shard, axis):
    copies = jnp.broadcast_to(shard, (lax.axis_size(axis), *shard.shape))
    return lax.all_to_all(copies, axis, split_axis=0, concat_axis=0, tiled=True)


def collect(shard, axis, dim):
    return joined_along(sent_to_all(shard, axis), dim)


def taken_together(shard, axis):
    return sent_to_all(shard, axis).max(axis=0)


def side_by_side(arrays, axis, dim, along):
    columns = [a.reshape(*a.shape[:along], -1) for a in arrays]
    both = jnp.concatenate(columns, axis=along)
    filled, at, finished = (lax.psum_scatter(both, axis, scatter_dimension=dim, tiled=True), 0, [])
    for a, column in zip(arrays, columns):
        slab = filled[..., at : at + column.shape[along]]
        finished.append(slab.reshape(*slab.shape[:along], *a.shape[along:]))
        at += column.shape[along]
    return tuple(finished)


def cut_along(shard, dim, length):
    before, after = (shard.shape[:dim], shard.shape[dim + 1 :])
    return jnp.moveaxis(shard.reshape(*before, length, -1, *after), dim, 0)


def sent_and_summed(shard, axis, dim):
    pieces = cut_along(shard, dim, lax.axis_size(axis))
    arrived = lax.all_to_all(pieces, axis, split_axis=0, concat_axis=0, tiled=True)
    return arrived.sum(axis=0)


def over_copies(shard, axis):
    everything = sent_to_all(shard, axis)
    return jnp.sum(everything, axis=0)


def sent_together(arrays, axis, dim, along):
    both = jnp.concatenate(arrays, axis=along)
    filled, at, finished = (lax.all_gather(both, axis, axis=dim, tiled=True), 0, [])
    for a in arrays:
        finished.append(lax.slice_in_dim(filled, at, at + a.shape[along], axis=along))
        at += a.shape[along]
    return tuple(finished)


def row_norm(values, gain_values, epsilon):
    meansq = jnp.mean(values * values, axis=-1, keepdims=True)
    return values * lax.rsqrt(meansq + epsilon) * gain_values


def per_device(
    patch_hidden,
    queries,
    new_keys,
    new_values,
    cache_keys,
    cache_values,
    cache_request,
    new_request,
    out_weight,
    norm_gain,
    dec_kv_weight,
    dec_query_weight,
    query_gain,
    key_gain,
    dec_out_weight,
    byte_states,
    byte_patch,
):
    new_rows, local_heads, head_size = queries.shape
    cache_rows = cache_keys.shape[0]
    total_rows = new_request.shape[0]
    ctx_index = lax.axis_index("ctx")
    head_index = lax.axis_index("head")
    first_new = ctx_index * new_rows
    all_keys = jnp.transpose(jnp.concatenate([cache_keys, new_keys], 0), (1, 0, 2))
    all_values = jnp.transpose(jnp.concatenate([cache_values, new_values], 0), (1, 0, 2))
    own_request = lax.dynamic_slice_in_dim(new_request, first_new, new_rows)
    local_request = jnp.concatenate([cache_request, own_request])
    local_position = jnp.concatenate(
        [jnp.full((cache_rows,), -1, jnp.int32), first_new + jnp.arange(new_rows, dtype=jnp.int32)]
    )
    key_low = jnp.minimum(cache_request[0], own_request[0])
    key_high = jnp.maximum(cache_request[cache_rows - 1], own_request[new_rows - 1])
    score_scale = head_size ** (-0.5)

    def partial_piece(portion):
        row_count = portion.shape[0]
        piece_index = jnp.arange(row_count, dtype=jnp.int32)
        visible = (local_request[None, :] == new_request[:, None]) & (
            local_position[None, :] <= piece_index[:, None]
        )

        def one_head(inputs):
            query_head, key_head, value_head = inputs
            scores = (
                jnp.einsum("qd,kd->qk", query_head, key_head, preferred_element_type=jnp.float32)
                * score_scale
            )
            highest = jnp.max(jnp.where(visible, scores, -1e30), axis=1)
            weights = jnp.where(visible, jnp.exp(scores - highest[:, None]), 0.0)
            mixed_rows = jnp.dot(
                weights.astype(jnp.bfloat16), value_head, preferred_element_type=jnp.float32
            )
            return (mixed_rows, jnp.sum(weights, axis=1), highest)

        return lax.map(one_head, (jnp.transpose(portion, (1, 0, 2)), all_keys, all_values))

    portion = collect(queries, "ctx", 0)
    offset = jnp.int32(0)
    row_count = portion.shape[0]
    request_low = new_request[offset]
    request_high = new_request[offset + row_count - 1]
    touches = (request_low <= key_high) & (request_high >= key_low)
    empty_part = (
        jnp.zeros((local_heads, row_count, head_size), jnp.float32),
        jnp.zeros((local_heads, row_count), jnp.float32),
        jnp.full((local_heads, row_count), -1e30, jnp.float32),
    )
    pieces = lax.cond(touches, lambda: partial_piece(portion), lambda: empty_part)
    partial_out, partial_total, partial_max = tuple((part_values for part_values in pieces))
    highest = taken_together(partial_max, "ctx")
    factor = jnp.exp(partial_max - highest)
    summed_out, summed_total = side_by_side(
        (partial_out * factor[..., None], partial_total * factor), "ctx", 1, 2
    )
    attended = (summed_out / summed_total[..., None]).astype(jnp.bfloat16)
    flattened = jnp.transpose(attended, (1, 0, 2)).reshape(new_rows, local_heads * head_size)
    head_terms = jnp.dot(
        flattened,
        out_weight.reshape(local_heads * head_size, -1),
        preferred_element_type=jnp.float32,
    )
    model_width = head_terms.shape[1]
    slice_width = patch_hidden.shape[1]
    projected = sent_and_summed(head_terms, "head", 1)
    patch_out = (patch_hidden.astype(jnp.float32) + projected).astype(jnp.bfloat16)
    widened = patch_out.astype(jnp.float32)
    squares = over_copies(jnp.sum(widened * widened, axis=1), "head")
    gain_part = lax.dynamic_slice_in_dim(norm_gain, head_index * slice_width, slice_width)
    normed_part = (widened * lax.rsqrt(squares / model_width + 1e-05)[:, None] * gain_part).astype(
        jnp.bfloat16
    )
    normed = collect(normed_part, "head", 1)
    dec_width = dec_kv_weight.shape[2]
    dec_heads = dec_width // DEC_DH
    patch_proj = jnp.dot(
        normed,
        dec_kv_weight.reshape(dec_kv_weight.shape[0], 2 * dec_width),
        preferred_element_type=jnp.float32,
    )
    patch_keys = row_norm(
        patch_proj[:, :dec_width].reshape(new_rows, dec_heads, DEC_DH), key_gain, 1e-06
    ).astype(jnp.bfloat16)
    patch_values = (
        patch_proj[:, dec_width:].astype(jnp.bfloat16).reshape(new_rows, dec_heads, DEC_DH)
    )
    byte_rows = byte_states.shape[0]
    query_proj = jnp.dot(byte_states, dec_query_weight, preferred_element_type=jnp.float32).reshape(
        byte_rows, dec_heads, DEC_DH
    )
    byte_query = row_norm(query_proj, query_gain, 1e-06).astype(jnp.bfloat16)
    table_index = jnp.arange(total_rows, dtype=jnp.int32)
    owner_table = table_index[None, :] == byte_patch[:, None]
    byte_request = jnp.sum(jnp.where(owner_table, new_request[None, :], 0), axis=1)
    dec_scale = DEC_DH ** (-0.5)
    piece_keys, piece_values = sent_together((patch_keys, patch_values), "ctx", 0, 1)
    row_count = piece_keys.shape[0]
    patch_index = jnp.arange(row_count, dtype=jnp.int32)
    visible = (new_request[None, :] == byte_request[:, None]) & (
        patch_index[None, :] <= byte_patch[:, None]
    )
    scores = (
        jnp.einsum("bhd,jhd->hbj", byte_query, piece_keys, preferred_element_type=jnp.float32)
        * dec_scale
    )
    weights = jnp.where(visible[None], jnp.exp(scores), 0.0)
    mixed_rows = jnp.einsum(
        "hbj,jhd->bhd",
        weights.astype(jnp.bfloat16),
        piece_values,
        preferred_element_type=jnp.float32,
    )
    denominator = jnp.transpose(jnp.sum(weights, axis=2))
    byte_mixed = (
        (mixed_rows / denominator[..., None]).astype(jnp.bfloat16).reshape(byte_rows, dec_width)
    )
    byte_terms = jnp.dot(byte_mixed, dec_out_weight, preferred_element_type=jnp.float32)
    byte_sum = sent_and_summed(byte_terms, "head", 1)
    out_width = byte_sum.shape[1]
    own_states = lax.dynamic_slice_in_dim(byte_states, head_index * out_width, out_width, 1)
    byte_out = (own_states.astype(jnp.float32) + byte_sum).astype(jnp.bfloat16)
    return (patch_out, byte_out)


def solution(mesh):
    placed = (
        P("ctx", "head"),
        P("ctx", "head", None),
        P("ctx", "head", None),
        P("ctx", "head", None),
        P("ctx", "head", None),
        P("ctx", "head", None),
        P("ctx"),
        P(),
        P("head", None, None),
        P(),
        P(None, None, "head"),
        P(None, "head"),
        P(),
        P(),
        P("head", None),
        P("ctx", None),
        P("ctx"),
    )
    return jax.shard_map(
        per_device,
        mesh=mesh,
        in_specs=placed,
        out_specs=(P("ctx", "head"), P("ctx", "head")),
        check_vma=False,
    )
```

profile of v0, /device:TPU:1, one launch (start us, length us, event | category | flops | bytes accessed | tf_op | source)
XLA Modules:
  0.0 466.5 jit_solution(3300536636312795367)
XLA Ops:
  10.0 11.3 %all-to-all-start = ((bf16[32,64,4,128]{3,1,2,0:T(8,128)(2,1)}), bf16[32,64,4,128]{3,1,2,0:T(8,128)(2,1)S(1)}, u32[]{:S(2)}, u32[]{:S(2)}) async-start(bf16[32,64,4,128]{3,1,2,0:T(8,128)(2,1)} %broadcast_in_dim.77), calls=%async_computation | async-start | bytes 4194304 | tf_op jit(solution)/shard_map/all_to_all | solution.py:17
  29.3 42.1 %all-to-all-done = bf16[32,64,4,128]{3,1,2,0:T(8,128)(2,1)S(1)} async-done(((bf16[32,64,4,128]{3,1,2,0:T(8,128)(2,1)}), bf16[32,64,4,128]{3,1,2,0:T(8,128)(2,1)S(1)}, u32[]{:S(2)}, u32[]{:S(2)}) %all-to-all-start) | async-done | bytes 2097184 | tf_op jit(solution)/shard_map/all_to_all | solution.py:17
  71.4 69.7 %conditional.1 = (f32[4,2048,128]{2,1,0:T(8,128)}, f32[4,2048]{1,0:T(4,128)}, f32[4,2048]{1,0:T(4,128)}) conditional(s32[]{:T(128)} %bitcast.2, () %tuple.24, (bf16[32,64,4,128]{3,1,2,0:T(8,128)(2,1)S(1)}, s32[1088]{0:T(1024)S(1)}, s32[2048]{0:T(1024)S(1)}, s32[]{:T(128)}, s32[64]{0:T(128)S(1)}, /*index=5*/bf16[4,1088,128]{2,1,0:T(8,128)(2,1)S(1)}, ...), branch_computations={%region_0.0_spmd, %region_1.6_spmd} | conditional | flops 1180954624 | bytes 68845856 | solution.py:138
  72.9 68.1 %while.19 = (s32[]{:T(128)}, f32[4,2048,128]{2,1,0:T(8,128)}, f32[4,2048]{1,0:T(4,128)}, f32[4,2048]{1,0:T(4,128)}, bf16[4,2048,128]{2,1,0:T(8,128)(2,1)}, /*ind...) while((s32[]{:T(128)}, f32[4,2048,128]{2,1,0:T(8,128)}, ...), condition=%wide.region_5.5_spmd.clone, body=%wide.region_2.4_spmd.clone.sunk | while | flops 1180954624 | bytes 64646296 | solution.py:125
  81.2 7.4 %fusion.71 = f32[4,2048,128]{2,1,0:T(8,128)} fusion(f32[4,2048,128]{2,1,0:T(8,128)} %get-tuple-element.265, s32[]{:T(128)} %get-tuple-element.264, f32[2048,1088]{0,1:T(8,128)} %copy-done.1, s32[1088]{0:T(1024)S(1)} %get-tuple-element.285, s32[2048]{0:T(1024)S(1)} %get-tuple-element.283, f32[2048]{0:T(1024)S(1)} %get-tuple-element.251, ...), kind=kOutput, calls=%fused_computation.10.clone.1 | convolution fusion | flops 583794688 | bytes 10266112 | tf_op jit(solution)/shard_map/cond/branch_1_fun/while/body/eval_jaxpr/dot_general | solution.py:120
  90.0 3.4 select_reduce_fusion.3
  98.2 7.4 %fusion.71 = f32[4,2048,128]{2,1,0:T(8,128)} fusion(f32[4,2048,128]{2,1,0:T(8,128)} %get-tuple-element.265, s32[]{:T(128)} %get-tuple-element.264, f32[2048,1088]{0,1:T(8,128)} %copy-done.1, s32[1088]{0:T(1024)S(1)} %get-tuple-element.285, s32[2048]{0:T(1024)S(1)} %get-tuple-element.283, f32[2048]{0:T(1024)S(1)} %get-tuple-element.251, ...), kind=kOutput, calls=%fused_computation.10.clone.1 | convolution fusion | flops 583794688 | bytes 10266112 | tf_op jit(solution)/shard_map/cond/branch_1_fun/while/body/eval_jaxpr/dot_general | solution.py:120
  107.0 3.4 select_reduce_fusion.3
  115.2 7.4 %fusion.71 = f32[4,2048,128]{2,1,0:T(8,128)} fusion(f32[4,2048,128]{2,1,0:T(8,128)} %get-tuple-element.265, s32[]{:T(128)} %get-tuple-element.264, f32[2048,1088]{0,1:T(8,128)} %copy-done.1, s32[1088]{0:T(1024)S(1)} %get-tuple-element.285, s32[2048]{0:T(1024)S(1)} %get-tuple-element.283, f32[2048]{0:T(1024)S(1)} %get-tuple-element.251, ...), kind=kOutput, calls=%fused_computation.10.clone.1 | convolution fusion | flops 583794688 | bytes 10266112 | tf_op jit(solution)/shard_map/cond/branch_1_fun/while/body/eval_jaxpr/dot_general | solution.py:120
  124.0 3.4 select_reduce_fusion.3
  132.2 7.4 %fusion.71 = f32[4,2048,128]{2,1,0:T(8,128)} fusion(f32[4,2048,128]{2,1,0:T(8,128)} %get-tuple-element.265, s32[]{:T(128)} %get-tuple-element.264, f32[2048,1088]{0,1:T(8,128)} %copy-done.1, s32[1088]{0:T(1024)S(1)} %get-tuple-element.285, s32[2048]{0:T(1024)S(1)} %get-tuple-element.283, f32[2048]{0:T(1024)S(1)} %get-tuple-element.251, ...), kind=kOutput, calls=%fused_computation.10.clone.1 | convolution fusion | flops 583794688 | bytes 10266112 | tf_op jit(solution)/shard_map/cond/branch_1_fun/while/body/eval_jaxpr/dot_general | solution.py:120
  142.0 32.6 %all_to_all.31 = f32[32,4,2048]{2,1,0:T(4,128)S(1)} all-to-all(f32[32,4,2048]{2,1,0:T(4,128)S(1)} %broadcast_in_dim.78), channel_id=1, replica_groups=mesh['ctx'=32,'head'=8] {'ctx'}, dimensions={0} | all-to-all | bytes 2097152 | tf_op jit(solution)/shard_map/all_to_all | solution.py:17
  178.3 3.9 broadcast_multiply_fusion
  182.2 3.9 pad_maximum_fusion
  186.1 6.5 %copy.95 = bf16[4096,512]{1,0:T(8,128)(2,1)} copy(bf16[4096,512]{0,1:T(8,128)(2,1)} %bitcast.81) | data formatting | bytes 8388608 | tf_op jit(solution)/shard_map/dot_general | solution.py:147
  192.6 117.5 %reduce-scatter.2.cloned.1.call-done = f32[4,64,129]{2,1,0:T(8,128)} async-done(((f32[4,2048,129]{2,1,0:T(8,128)}), f32[4,64,129]{2,1,0:T(8,128)}) %reduce-scatter.2.cloned.1.call-update) | async-done | bytes 132112 | tf_op jit(solution)/shard_map/reduce_scatter | solution.py:31
  312.3 3.6 convolution_bitcast_fusion.1
  315.9 18.7 %all_to_all.32 = f32[8,64,512]{2,1,0:T(8,128)S(1)} all-to-all(f32[8,64,512]{2,1,0:T(8,128)S(1)} %convolution_bitcast_fusion.1), channel_id=1, replica_groups=mesh['ctx'=32,'head'=8] {'head'}, dimensions={0} | all-to-all | bytes 2097152 | tf_op jit(solution)/shard_map/all_to_all | solution.py:46
  339.5 5.5 %all-to-all-done.3 = f32[8,1,64]{2,1,0:T(1,128)S(1)} async-done(((f32[8,1,64]{2,1,0:T(1,128)}), f32[8,1,64]{2,1,0:T(1,128)S(1)}, u32[]{:S(2)}, u32[]{:S(2)}) %all-to-all-start.3) | async-done | bytes 2080 | tf_op jit(solution)/shard_map/all_to_all | solution.py:17
  345.2 11.1 %all_to_all.33 = bf16[8,64,512]{2,1,0:T(8,128)(2,1)S(1)} all-to-all(bf16[8,64,512]{2,1,0:T(8,128)(2,1)S(1)} %broadcast_in_dim.80), channel_id=1, replica_groups=mesh['ctx'=32,'head'=8] {'head'}, dimensions={0} | all-to-all | bytes 1048576 | tf_op jit(solution)/shard_map/all_to_all | solution.py:17
  361.4 67.7 %all-gather.2.cloned.1.call-done = bf16[2048,4,64]{2,1,0:T(4,128)(2,1)} async-done(((bf16[64,4,64]{2,1,0:T(4,128)(2,1)}), bf16[2048,4,64]{2,1,0:T(4,128)(2,1)}) %all-gather.2.cloned.1.call-update) | async-done | bytes 1048592 | tf_op jit(solution)/shard_map/all_gather | solution.py:57
  429.2 4.0 fusion.54
  437.0 6.1 %all-to-all-start.5 = ((f32[8,256,128]{2,1,0:T(8,128)}), f32[8,256,128]{2,1,0:T(8,128)S(1)}, u32[]{:S(2)}, u32[]{:S(2)}) async-start(f32[8,256,128]{2,1,0:T(8,128)} %convolution_bitcast_fusion), calls=%async_computation.6 | async-start | bytes 2097152 | tf_op jit(solution)/shard_map/all_to_all | solution.py:46
  443.1 15.9 %all-to-all-done.5 = f32[8,256,128]{2,1,0:T(8,128)S(1)} async-done(((f32[8,256,128]{2,1,0:T(8,128)}), f32[8,256,128]{2,1,0:T(8,128)S(1)}, u32[]{:S(2)}, u32[]{:S(2)}) %all-to-all-start.5) | async-done | bytes 1048608 | tf_op jit(solution)/shard_map/all_to_all | solution.py:46
  (108 shorter events, 58.0 us)
Async XLA Ops:
  7.2 353.2 %copy-start = (bf16[1024,128]{1,0:T(8,128)(2,1)S(1)}, bf16[1024,128]{1,0:T(8,128)(2,1)}, u32[]{:S(2)}) copy-start(bf16[1024,128]{1,0:T(8,128)(2,1)} %param.32) | copy-start | bytes 786436
  7.2 14.2 %copy-start.5 = (s32[2048]{0:T(1024)S(1)}, s32[2048]{0:T(1024)}, u32[]{:S(2)}) copy-start(s32[2048]{0:T(1024)} %param.28) | copy-start | bytes 24580
  7.2 14.3 %copy-start.11 = (s32[1024]{0:T(1024)S(1)}, s32[1024]{0:T(1024)}, u32[]{:S(2)}) copy-start(s32[1024]{0:T(1024)} %param.27) | copy-start | bytes 12292
  7.2 19.3 %copy-start.3 = (bf16[1024,4,128]{2,1,0:T(4,128)(2,1)S(1)}, bf16[1024,4,128]{2,1,0:T(4,128)(2,1)}, u32[]{:S(2)}) copy-start(bf16[1024,4,128]{2,1,0:T(4,128)(2,1)} %param.25) | copy-start | bytes 3145732
  10.0 18.0 %copy-start.8 = (bf16[64,4,128]{2,1,0:T(4,128)(2,1)S(1)}, bf16[64,4,128]{2,1,0:T(4,128)(2,1)}, u32[]{:S(2)}) copy-start(bf16[64,4,128]{2,1,0:T(4,128)(2,1)} %param.23) | copy-start | bytes 196612
  10.0 18.0 %copy-start.9 = (bf16[64,4,128]{2,1,0:T(4,128)(2,1)S(1)}, bf16[64,4,128]{2,1,0:T(4,128)(2,1)}, u32[]{:S(2)}) copy-start(bf16[64,4,128]{2,1,0:T(4,128)(2,1)} %param.24) | copy-start | bytes 196612
  10.0 61.3 %all-to-all-start = ((bf16[32,64,4,128]{3,1,2,0:T(8,128)(2,1)}), bf16[32,64,4,128]{3,1,2,0:T(8,128)(2,1)S(1)}, u32[]{:S(2)}, u32[]{:S(2)}) async-start(bf16[32,64,4,128]{3,1,2,0:T(8,128)(2,1)} %broadcast_in_dim.77), calls=%async_computation | async-start | bytes 4194304 | tf_op jit(solution)/shard_map/all_to_all | solution.py:17
  21.3 288.8 %reduce-scatter.2.cloned.1.call-start = ((), (), s32[]{:S(2)}) async-start(), calls=%async_computation.7 | async-start | bytes 8650752 | tf_op jit(solution)/shard_map/reduce_scatter | solution.py:31
  76.3 3.4 copy-start.1
  93.4 3.4 copy-start.1
  110.4 3.4 copy-start.1
  127.4 3.4 copy-start.1
  178.3 3.9 copy-start.2
  312.3 22.4 %copy-start.10 = (bf16[64,512]{1,0:T(8,128)(2,1)S(1)}, bf16[64,512]{1,0:T(8,128)(2,1)}, u32[]{:S(2)}) copy-start(bf16[64,512]{1,0:T(8,128)(2,1)} %param.21) | copy-start | bytes 196612
  334.6 24.3 %copy-start.13 = (f32[64]{0:T(128)S(1)}, f32[64]{0:T(128)}, u32[]{:S(2)}) copy-start(f32[64]{0:T(128)} %param.34) | copy-start | bytes 772
  334.6 25.2 %copy-start.6 = (bf16[128,1024]{1,0:T(8,128)(2,1)S(1)}, bf16[128,1024]{1,0:T(8,128)(2,1)}, u32[]{:S(2)}) copy-start(bf16[128,1024]{1,0:T(8,128)(2,1)} %param.35) | copy-start | bytes 786436
  334.6 25.4 %copy-start.12 = (s32[256]{0:T(256)S(1)}, s32[256]{0:T(256)}, u32[]{:S(2)}) copy-start(s32[256]{0:T(256)} %param.37) | copy-start | bytes 3076
  334.6 25.8 %copy-start.4 = (bf16[256,1024]{1,0:T(8,128)(2,1)S(1)}, bf16[256,1024]{1,0:T(8,128)(2,1)}, u32[]{:S(2)}) copy-start(bf16[256,1024]{1,0:T(8,128)(2,1)} %param.36) | copy-start | bytes 1572868
  334.8 26.7 %copy-start.7 = (bf16[64,512]{1,0:T(8,128)(2,1)}, bf16[64,512]{1,0:T(8,128)(2,1)S(1)}, u32[]{:S(2)}) copy-start(bf16[64,512]{1,0:T(8,128)(2,1)S(1)} %get-tuple-element.166) | copy-start | bytes 196612
  335.4 9.7 %all-to-all-start.3 = ((f32[8,1,64]{2,1,0:T(1,128)}), f32[8,1,64]{2,1,0:T(1,128)S(1)}, u32[]{:S(2)}, u32[]{:S(2)}) async-start(f32[8,1,64]{2,1,0:T(1,128)} %broadcast_in_dim.79), calls=%async_computation.4 | async-start | bytes 8192 | tf_op jit(solution)/shard_map/all_to_all | solution.py:17
  338.7 90.5 %all-gather.2.cloned.1.call-start = ((), (), s32[]{:S(2)}) async-start(), calls=%async_computation.8 | async-start | bytes 2162688 | tf_op jit(solution)/shard_map/all_gather | solution.py:57
  356.4 76.8 %copy-start.14 = (f32[64]{0:T(128)S(1)}, f32[64]{0:T(128)}, u32[]{:S(2)}) copy-start(f32[64]{0:T(128)} %param.33) | copy-start | bytes 772
  437.0 22.0 %all-to-all-start.5 = ((f32[8,256,128]{2,1,0:T(8,128)}), f32[8,256,128]{2,1,0:T(8,128)S(1)}, u32[]{:S(2)}, u32[]{:S(2)}) async-start(f32[8,256,128]{2,1,0:T(8,128)} %convolution_bitcast_fusion), calls=%async_computation.6 | async-start | bytes 2097152 | tf_op jit(solution)/shard_map/all_to_all | solution.py:46
Sparse Core Ops, SparseCore 0:
  186.2 123.8 reduce-scatter.1
  359.9 69.2 all-gather.1
where the time goes:
time: 468 us; the launch traced here: 467 us
  waiting for transfers between devices  249 us (53%)
  blocking collectives  62.4 us (13%)
  matrix products  52.9 us (11%)
  local copies, waits for them, and re-layouts  37.3 us (8%)
  other arithmetic  26 us (6%)
  starting transfers between devices  20.8 us (4%)
  between operations  18.3 us (4%)
    reduce_scatter x1, waiting for transfers between devices, side_by_side(): lax.psum_scatter(both, axis, scatter_dimension=dim, tiled=True)  118 us
    all_gather x1, waiting for transfers between devices, sent_together(): lax.all_gather(both, axis, axis=dim, tiled=True)  67.7 us
    all_to_all x2, waiting for transfers between devices, sent_to_all(): return lax.all_to_all(copies, axis, split_axis=0, concat_axis=0, tiled=True)  47.7 us
    all_to_all x2, blocking collectives, sent_to_all(): return lax.all_to_all(copies, axis, split_axis=0, concat_axis=0, tiled=True)  43.7 us
    dot_general x4, matrix products, one_head(): jnp.dot(weights.astype(jnp.bfloat16), value_head, preferred_element_type=...  29.6 us
    all_to_all x1, blocking collectives, sent_and_summed(): lax.all_to_all(pieces, axis, split_axis=0, concat_axis=0, tiled=True)  18.7 us
    all_to_all x1, waiting for transfers between devices, sent_and_summed(): lax.all_to_all(pieces, axis, split_axis=0, concat_axis=0, tiled=True)  15.9 us
    all_to_all x2, starting transfers between devices, sent_to_all(): return lax.all_to_all(copies, axis, split_axis=0, concat_axis=0, tiled=True)  14.6 us
  transfers between devices with their start and end apart: 5, of which 5 were waited for; matrix products, arithmetic and copies ran while one was open for 3% of the time, Pallas kernels for 0%

commit v1 on v0

v1 whole, which is shorter than its diff:
```python
import functools

import jax
import jax.numpy as jnp
from jax import lax
from jax.experimental import pallas as pl
from jax.experimental.pallas import tpu as pltpu
from jax.sharding import PartitionSpec as P

MESH = pl.DeviceIdType.MESH
VMEM = pltpu.VMEM
F32 = jnp.float32
BF16 = jnp.bfloat16
LOW = -1e20
HIDE = -1e30
LOG2E = 1.4426950408889634


def in_vmem():
    return pl.BlockSpec(memory_space=pltpu.VMEM)


def in_place():
    return pl.BlockSpec(memory_space=pl.ANY)


class Place:
    def __init__(self, zn):
        c = lax.axis_index("ctx")
        self.c = c
        self.zn = zn
        self.z = lax.div(c, 4)
        self.yl = lax.rem(lax.div(c, 2), 2)
        self.k = lax.rem(c, 2)
        low = lax.rem(c, 4)
        self.core_peer = c + 1 - 2 * self.k
        self.y_peer = c + 2 - 4 * self.yl
        self.right = self.around(1) * 4 + low
        self.left = self.around(-1) * 4 + low

    def around(self, step):
        return lax.rem(self.z + (step + 2 * self.zn), self.zn)


class Sends:
    def __init__(self, send_sem, recv_sem):
        self.send_sem, self.recv_sem, self.used = send_sem, recv_sem, 0

    def make(self, src, dst, device):
        at = self.used
        self.used += 1
        return pltpu.make_async_remote_copy(
            src_ref=src,
            dst_ref=dst,
            send_sem=self.send_sem.at[at],
            recv_sem=self.recv_sem.at[at],
            device_id=device,
            device_id_type=MESH,
        )


def greet(devices):
    barrier = pltpu.get_barrier_semaphore()
    for device in devices:
        pl.semaphore_signal(barrier, inc=1, device_id=device, device_id_type=MESH)
    pl.semaphore_wait(barrier, len(devices))


def ring_gather(sends, place, buffer, rows, from_y):
    zn = place.zn
    far, near = zn // 2, zn - 1 - zn // 2

    def slot(z, y):
        start = pl.multiple_of((z * 2 + y) * rows, rows)
        return buffer.at[pl.ds(start, rows), :]

    streams = ((place.yl, far, near), (1 - place.yl, near, far))
    made = {}
    for step in range(max(far, near)):
        for which, (y, to_right, to_left) in enumerate(streams):
            if step == 0 and which == 1:
                from_y.wait_recv()
            for way, count, device in ((1, to_right, place.right), (-1, to_left, place.left)):
                if step >= count:
                    continue
                if step > 0:
                    made[which, way, step - 1].wait_recv()
                piece = slot(place.around(-way * step), y)
                copy = sends.make(piece, piece, {"ctx": device})
                copy.start()
                made[which, way, step] = copy
    if not made:
        from_y.wait_recv()
    for (which, way, step), copy in made.items():
        if (which, way, step + 1) not in made:
            copy.wait_recv()
    for copy in made.values():
        copy.wait_send()


def spread(zn, q_ref, k_ref, v_ref, cr_ref, nr_ref, qg, kc, vc, bounds, cr_both, send_sem, recv_sem, local_sem):
    place = Place(zn)
    sends = Sends(send_sem, recv_sem)
    k, z, yl = place.k, place.z, place.yl
    new = q_ref.shape[0]
    width = qg.shape[1]
    cached = k_ref.shape[0] - new
    greet([{"ctx": d} for d in (place.core_peer, place.y_peer, place.right, place.left)])
    peer = {"ctx": place.core_peer}
    own_cols = pl.ds(pl.multiple_of(k * width, width), width)
    peer_cols = pl.ds(pl.multiple_of((1 - k) * width, width), width)
    chip = z * 2 + yl
    chip_rows = pl.ds(pl.multiple_of(chip * 2 * new, 2 * new), 2 * new)
    q_rows = pl.ds(pl.multiple_of(place.c * new, new), new)
    q_send = sends.make(q_ref.at[:, peer_cols], qg.at[q_rows, :], peer)
    q_send.start()
    q_local = pltpu.make_async_copy(q_ref.at[:, own_cols], qg.at[q_rows, :], local_sem.at[0])
    q_local.start()
    cr_send = sends.make(cr_ref, cr_both.at[k], peer)
    cr_send.start()
    swaps, locals_ = [], []
    old_from, new_from = pl.ds(0, cached), pl.ds(cached, new)
    old_to = pl.ds(pl.multiple_of(k * cached, cached), cached)
    new_to = pl.ds(pl.multiple_of(2 * cached + k * new, new), new)
    for src, dst in ((k_ref, kc), (v_ref, vc)):
        for rows_from, rows_to in ((old_from, old_to), (new_from, new_to)):
            swaps.append(sends.make(src.at[rows_from, peer_cols], dst.at[rows_to, :], peer))
            locals_.append(
                pltpu.make_async_copy(
                    src.at[rows_from, own_cols], dst.at[rows_to, :], local_sem.at[1 + len(locals_)]
                )
            )
    q_local.wait()
    q_send.wait_recv()
    mine = qg.at[chip_rows, :]
    to_y = sends.make(mine, mine, {"ctx": place.y_peer})
    to_y.start()
    for copy in swaps:
        copy.start()
    for copy in locals_:
        copy.start()
    cr_send.wait_recv()
    cr_both[pl.ds(k, 1)] = cr_ref[...][None]
    ring_gather(sends, place, qg, 2 * new, to_y)
    held = cr_both[...]
    mates = nr_ref[...]
    total = mates.shape[1]
    zero = jnp.zeros((1, total), F32)
    low, high, start = zero, zero, zero
    below = jnp.zeros((1, 1), F32)
    for r in range(8):
        ones = jnp.where(held <= r, 1.0, 0.0)
        upto = jnp.sum(jnp.sum(ones, axis=0), axis=(0, 1), keepdims=True)
        first = jnp.sum(jnp.where(mates < r, 1.0, 0.0), axis=1, keepdims=True)
        here = mates == r
        low = jnp.where(here, below, low)
        high = jnp.where(here, upto, high)
        start = jnp.where(here, first, start)
        below = upto
    shift = chip * 2 * new
    index = lax.broadcasted_iota(jnp.int32, (1, total), 1)
    bounds[0:1, :] = low.astype(jnp.int32)
    bounds[1:2, :] = high.astype(jnp.int32)
    bounds[2:3, :] = start.astype(jnp.int32) - shift
    bounds[3:4, :] = index - (shift - 1)
    bounds[4:8, :] = jnp.zeros((4, total), jnp.int32)
    for copy in locals_:
        copy.wait()
    for copy in swaps:
        copy.wait()
    q_send.wait_send()
    cr_send.wait_send()
    to_y.wait_send()


def attend(cached, block, scale, q_ref, k_ref, v_ref, bv_ref, bs_ref, o_ref, m_s, l_s, acc_s):
    rows = q_ref.shape[0]
    new = k_ref.shape[0] - cached
    q0 = pl.program_id(0) * rows
    last = q0 + rows - 1
    heads, dim = acc_s.shape[0], acc_s.shape[1]
    m_s[...] = jnp.full_like(m_s, LOW).astype(BF16).astype(F32)
    l_s[...] = jnp.zeros_like(l_s)
    acc_s[...] = jnp.zeros_like(acc_s)

    def add(first, count, base, low, high):
        for h in range(heads):
            cols = slice(h * dim, (h + 1) * dim)
            scores = lax.dot_general(
                k_ref[pl.ds(first, count), cols],
                q_ref[:, cols],
                (((1,), (1,)), ((), ())),
                preferred_element_type=F32,
            )
            if low is not None:
                at = lax.broadcasted_iota(jnp.int32, scores.shape, 0) + base
                scores = jnp.where((at >= low) & (at < high), scores, HIDE)
            top = jnp.max(scores, axis=0, keepdims=True) * scale
            m_old = m_s[h]
            m_new = jnp.maximum(m_old, top.astype(BF16).astype(F32))
            weights = jnp.exp2(scores * scale - m_new)
            fade = jnp.exp2(m_old - m_new)
            m_s[h] = m_new
            l_s[h] = l_s[h] * fade + jnp.sum(weights, axis=0, keepdims=True)
            acc_s[h] = acc_s[h] * fade + lax.dot_general(
                v_ref[pl.ds(first, count), cols],
                weights.astype(BF16),
                (((0,), (0,)), ((), ())),
                preferred_element_type=F32,
            )

    low_first, low_last = bs_ref[0, q0], bs_ref[0, last]
    high_first, high_last = bs_ref[1, q0], bs_ref[1, last]
    begin = lax.div(low_first, block)
    end = jnp.where(high_last > low_first, lax.div(high_last + block - 1, block), begin)

    def one_block(b, carry):
        first = pl.multiple_of(b * block, block)
        whole = (low_last <= first) & (high_first >= first + block)

        @pl.when(whole)
        def _():
            add(first, block, first, None, None)

        @pl.when(jnp.logical_not(whole))
        def _():
            add(first, block, first, bv_ref[0:1, :], bv_ref[1:2, :])

        return carry

    lax.fori_loop(begin, end, one_block, 0)

    @pl.when((bs_ref[3, last] > 0) & (bs_ref[2, q0] < new))
    def _():
        add(cached, new, 0, bv_ref[2:3, :], bv_ref[3:4, :])

    for h in range(heads):
        pack(o_ref.at[0, h], acc_s[h], m_s[h], l_s[h])


def pack(ref, out, top, total):
    dim = out.shape[0]
    ref[0:dim, :] = out.astype(BF16)
    coarse = total.astype(BF16).astype(F32)
    row = lax.broadcasted_iota(jnp.int32, (16, out.shape[1]), 0)
    tail = jnp.where(row == 0, top, jnp.where(row == 1, coarse, jnp.where(row == 2, total - coarse, 0.0)))
    ref[dim : dim + 16, :] = tail.astype(BF16)


def unpack(ref):
    value = ref[...]
    dim = value.shape[0] - 16
    tail = value[dim:, :].astype(F32)
    return value[:dim, :].astype(F32), tail[0:1, :], tail[1:2, :] + tail[2:3, :]


def merged(parts):
    top = parts[0][1]
    for part in parts[1:]:
        top = jnp.maximum(top, part[1])
    out, total = 0.0, 0.0
    for o, m, l in parts:
        factor = jnp.exp2(m - top)
        out = out + o * factor
        total = total + l * factor
    return out, top, total


def head_norm(values, gain, half):
    lane = lax.broadcasted_iota(jnp.int32, values.shape, 1)
    first = lane < half
    squares = values * values
    s0 = jnp.sum(jnp.where(first, squares, 0.0), axis=1, keepdims=True)
    s1 = jnp.sum(jnp.where(first, 0.0, squares), axis=1, keepdims=True)
    return values * lax.rsqrt(jnp.where(first, s0, s1) / half + 1e-6) * gain


def finish(
    zn, hn, part, hidden, w_hbm, dkv_hbm, gain_ref, kgain_ref, qgain_ref, dqw_ref, dow_ref, states_ref, bp_ref, nr_ref,
    patch_out, byte_out,
    w_ref, dkv_ref, ring_in, ring_out, y_in, y_out, att_t, att, rs_out, rs_in, ag_in, kv_tile, kvg, bq_tile, bq,
    bp_both, mix_tile, mix, bs_out, bs_in, send_sem, recv_sem, local_sem,
):
    place = Place(zn)
    sends = Sends(send_sem, recv_sem)
    k, z, yl = place.k, place.z, place.yl
    me = lax.axis_index("head")
    peer, beside = {"ctx": place.core_peer}, {"ctx": place.y_peer}
    others = [lax.rem(me + i, hn) for i in range(1, hn)]
    sources = [lax.rem(me + hn - i, hn) for i in range(1, hn)]
    greet(
        [{"ctx": d} for d in (place.core_peer, place.y_peer, place.right, place.left)]
        + [{"head": d} for d in others]
    )
    w_load = pltpu.make_async_copy(w_hbm, w_ref, local_sem.at[0])
    w_load.start()
    dkv_load = pltpu.make_async_copy(dkv_hbm, dkv_ref, local_sem.at[1])
    dkv_load.start()
    pending = []
    new, slice_width = hidden.shape
    heads = part.shape[1]
    dim = part.shape[2] - 16

    bp_send = sends.make(bp_ref, bp_both.at[k], peer)
    bp_send.start()

    far, near = zn // 2, zn - 1 - zn // 2
    counts = [(far, near) if h % 2 == 0 else (near, far) for h in range(heads)]
    made = {}
    for step in range(max(far, near)):
        for h in range(heads):
            for way, device in ((0, place.right), (1, place.left)):
                count = counts[h][way]
                if step >= count:
                    continue
                ahead = count - step
                target = place.around(ahead if way == 0 else -ahead)
                if step == 0:
                    src = part.at[target, h]
                else:
                    made[h, way, step - 1].wait_recv()
                    src = ring_out.at[h, way, step]
                    pack(src, *merged([unpack(part.at[target, h]), unpack(ring_in.at[h, way, step - 1])]))
                copy = sends.make(src, ring_in.at[h, way, step], {"ctx": device})
                copy.start()
                made[h, way, step] = copy
        if step == 0:
            proj = jnp.dot(states_ref[...], dqw_ref[...], preferred_element_type=F32)
            half = proj.shape[1] // 2
            normed = head_norm(proj, qgain_ref[...], half)
            lane = lax.broadcasted_iota(jnp.int32, normed.shape, 1)
            bq_tile[0] = jnp.where(lane < half, normed, 0.0).astype(BF16)
            bq_tile[1] = jnp.where(lane < half, pltpu.roll(normed, half, 1), 0.0).astype(BF16)
            bytes_ = bq_tile.shape[1]
            byte_rows = pl.ds(pl.multiple_of(k * bytes_, bytes_), bytes_)
            bq_send = sends.make(bq_tile.at[1 - k], bq.at[byte_rows, :], peer)
            bq_send.start()
            bq[byte_rows, :] = bq_tile[k]
            pending += [bp_send, bq_send]
    y_cols = pl.ds(pl.multiple_of((1 - yl) * 2 * new, 2 * new), 2 * new)
    own_cols = pl.ds(pl.multiple_of(yl * 2 * new, 2 * new), 2 * new)
    for h in range(heads):
        got = [unpack(part.at[z, h])]
        for way in (0, 1):
            count = counts[h][way]
            if count:
                made[h, way, count - 1].wait_recv()
                got.append(unpack(ring_in.at[h, way, count - 1]))
        pack(y_out.at[h], *merged(got))
    y_send = sends.make(y_out.at[:, :, y_cols], y_in, beside)
    y_send.start()
    pending += list(made.values()) + [y_send]
    y_send.wait_recv()
    core_rows = heads * dim
    for h in range(heads):
        out, _, total = merged([unpack(y_out.at[h, :, own_cols]), unpack(y_in.at[h])])
        rows = pl.ds(pl.multiple_of(k * core_rows + h * dim, dim), dim)
        att_t[rows, :] = (out / total).astype(BF16)
    held = att_t.at[pl.ds(pl.multiple_of(k * core_rows, core_rows), core_rows), :]
    att_send = sends.make(held, held, peer)
    att_send.start()
    w_load.wait()
    att_send.wait_recv()
    pending.append(att_send)
    att[...] = att_t[...].T

    mine = att[pl.ds(pl.multiple_of(k * new, new), new), :]

    def columns_for(d):
        cols = pl.ds(pl.multiple_of(d * slice_width, slice_width), slice_width)
        return jnp.dot(mine, w_ref[:, cols], preferred_element_type=F32)

    rs_sends = []
    for i, d in enumerate(others):
        rs_out[i] = columns_for(d).astype(BF16)
        copy = sends.make(rs_out.at[i], rs_in.at[i], {"head": d})
        copy.start()
        rs_sends.append(copy)
    own = columns_for(me) + hidden[...].astype(F32)
    for i, copy in enumerate(rs_sends):
        copy.wait_recv()
        own = own + rs_in[i].astype(F32)
    rounded = own.astype(BF16)
    patch_out[...] = rounded
    ag_in[0] = rounded
    ag_sends = []
    for i, d in enumerate(others):
        copy = sends.make(ag_in.at[0], ag_in.at[1 + i], {"head": d})
        copy.start()
        ag_sends.append(copy)
    pending += rs_sends + ag_sends
    squares = 0.0
    for i in range(hn):
        if i:
            ag_sends[i - 1].wait_recv()
        wide = ag_in[i].astype(F32)
        squares = squares + jnp.sum(wide * wide, axis=1, keepdims=True)
    inverse = lax.rsqrt(squares / (hn * slice_width) + 1e-5)
    dkv_load.wait()
    proj = 0.0
    for i in range(hn):
        source = me if i == 0 else sources[i - 1]
        normed = (ag_in[i].astype(F32) * inverse * gain_ref[pl.ds(source, 1), :]).astype(BF16)
        rows = pl.ds(pl.multiple_of(source * slice_width, slice_width), slice_width)
        proj = proj + jnp.dot(normed, dkv_ref[rows, :], preferred_element_type=F32)
    width = proj.shape[1] // 2
    half = width // 2
    keys = head_norm(proj[:, :width], kgain_ref[...], half)
    values = proj[:, width:]
    lane = lax.broadcasted_iota(jnp.int32, keys.shape, 1)
    kv_tile[0] = jnp.where(lane < half, keys, pltpu.roll(values, half, 1)).astype(BF16)
    kv_tile[1] = jnp.where(lane < half, pltpu.roll(keys, half, 1), values).astype(BF16)
    kv_rows = pl.ds(pl.multiple_of(place.c * new, new), new)
    kv_send = sends.make(kv_tile.at[1 - k], kvg.at[kv_rows, :], peer)
    kv_send.start()
    kvg[kv_rows, :] = kv_tile[k]
    kv_send.wait_recv()
    chip = z * 2 + yl
    slot = kvg.at[pl.ds(pl.multiple_of(chip * 2 * new, 2 * new), 2 * new), :]
    kv_y = sends.make(slot, slot, beside)
    kv_y.start()
    pending += [kv_send, kv_y]

    bp_send.wait_recv()
    bp_both[pl.ds(k, 1)] = bp_ref[...][None]
    owner = jnp.concatenate([bp_both[0], bp_both[1]], axis=1)
    first = jnp.zeros(owner.shape, F32)
    mates = nr_ref[...]
    for r in range(1, 8):
        begins = jnp.sum(jnp.where(mates < r, 1.0, 0.0), axis=1, keepdims=True)
        first = jnp.where(owner.astype(F32) >= begins, begins, first)
    first = first.astype(jnp.int32)
    bq_send.wait_recv()
    ring_gather(sends, place, kvg, 2 * new, kv_y)

    queries = bq[...]
    block = min(512, kvg.shape[0])
    scale = half ** (-0.5) * LOG2E
    out, total = 0.0, 0.0
    for b in range(kvg.shape[0] // block):
        kv = kvg[b * block : (b + 1) * block, :]
        scores = lax.dot_general(kv, queries, (((1,), (1,)), ((), ())), preferred_element_type=F32)
        at = lax.broadcasted_iota(jnp.int32, scores.shape, 0) + b * block
        weights = jnp.where((at >= first) & (at <= owner), jnp.exp2(scores * scale), 0.0)
        total = total + jnp.sum(weights, axis=0, keepdims=True)
        out = out + lax.dot_general(
            kv, weights.astype(BF16), (((0,), (0,)), ((), ())), preferred_element_type=F32
        )
    mix_tile[...] = (out[half:, :] / total).astype(BF16)
    mix_rows = pl.ds(pl.multiple_of(k * half, half), half)
    bytes_ = states_ref.shape[0]
    theirs = pl.ds(pl.multiple_of((1 - k) * bytes_, bytes_), bytes_)
    ours = pl.ds(pl.multiple_of(k * bytes_, bytes_), bytes_)
    mix_send = sends.make(mix_tile.at[:, theirs], mix.at[mix_rows, :], peer)
    mix_send.start()
    mix[mix_rows, :] = mix_tile[:, ours]
    mix_send.wait_recv()
    pending.append(mix_send)
    mixed = mix[...]
    out_width = byte_out.shape[1]

    def byte_columns_for(d):
        cols = pl.ds(pl.multiple_of(d * out_width, out_width), out_width)
        return lax.dot_general(mixed, dow_ref[:, cols], (((0,), (0,)), ((), ())), preferred_element_type=F32)

    bs_sends = []
    for i, d in enumerate(others):
        bs_out[i] = byte_columns_for(d).astype(BF16)
        copy = sends.make(bs_out.at[i], bs_in.at[i], {"head": d})
        copy.start()
        bs_sends.append(copy)
    own_states = states_ref[:, pl.ds(pl.multiple_of(me * out_width, out_width), out_width)]
    own = byte_columns_for(me) + own_states.astype(F32)
    for i, copy in enumerate(bs_sends):
        copy.wait_recv()
        own = own + bs_in[i].astype(F32)
    byte_out[...] = own.astype(BF16)
    for copy in pending + bs_sends:
        copy.wait_send()


def per_device(
    zn,
    hn,
    patch_hidden,
    queries,
    new_keys,
    new_values,
    cache_keys,
    cache_values,
    cache_request,
    new_request,
    out_weight,
    norm_gain,
    dec_kv_weight,
    dec_query_weight,
    query_gain,
    key_gain,
    dec_out_weight,
    byte_states,
    byte_patch,
):
    new, heads, dim = queries.shape
    cached = cache_keys.shape[0]
    total = new_request.shape[0]
    pair = heads // 2 * dim
    all_keys = 2 * (cached + new)
    slice_width = patch_hidden.shape[1]
    flat_keys = jnp.concatenate([cache_keys, new_keys], 0).reshape(cached + new, heads * dim)
    flat_values = jnp.concatenate([cache_values, new_values], 0).reshape(cached + new, heads * dim)
    held = cache_request.reshape(8, cached // 8)
    mates = new_request.reshape(1, total)
    gather_copies = 8 + 2 * (zn - 1)
    gathered, keys, values, bounds = pl.pallas_call(
        functools.partial(spread, zn),
        out_shape=(
            jax.ShapeDtypeStruct((total, pair), BF16),
            jax.ShapeDtypeStruct((all_keys, pair), BF16),
            jax.ShapeDtypeStruct((all_keys, pair), BF16),
            jax.ShapeDtypeStruct((8, total), jnp.int32),
        ),
        in_specs=[in_vmem(), in_place(), in_place(), in_vmem(), in_vmem()],
        out_specs=(in_vmem(), in_place(), in_place(), in_vmem()),
        scratch_shapes=[
            VMEM((2, *held.shape), jnp.int32),
            pltpu.SemaphoreType.DMA((gather_copies,)),
            pltpu.SemaphoreType.DMA((gather_copies,)),
            pltpu.SemaphoreType.DMA((5,)),
        ],
        compiler_params=pltpu.CompilerParams(
            collective_id=0, has_side_effects=True, vmem_limit_bytes=24 * 2**20
        ),
        name="spread",
    )(queries.reshape(new, heads * dim), flat_keys, flat_values, held, mates)

    tile = 4 * new
    block = min(512, cached)
    partial = pl.pallas_call(
        functools.partial(attend, 2 * cached, block, dim ** (-0.5) * LOG2E),
        out_shape=jax.ShapeDtypeStruct((zn, heads // 2, dim + 16, tile), BF16),
        grid=(zn,),
        in_specs=[
            pl.BlockSpec((tile, pair), lambda t: (t, 0)),
            pl.BlockSpec((all_keys, pair), lambda t: (0, 0)),
            pl.BlockSpec((all_keys, pair), lambda t: (0, 0)),
            pl.BlockSpec((8, tile), lambda t: (0, t)),
            pl.BlockSpec(memory_space=pltpu.SMEM),
        ],
        out_specs=pl.BlockSpec((1, heads // 2, dim + 16, tile), lambda t: (t, 0, 0, 0)),
        scratch_shapes=[
            VMEM((heads // 2, 1, tile), F32),
            VMEM((heads // 2, 1, tile), F32),
            VMEM((heads // 2, dim, tile), F32),
        ],
        compiler_params=pltpu.CompilerParams(vmem_limit_bytes=32 * 2**20),
        name="attend",
    )(gathered, keys, values, bounds, bounds)

    kv_rows = dec_kv_weight.shape[0]
    dec_width = dec_kv_weight.shape[2]
    bytes_ = byte_states.shape[0]
    out_width = dec_out_weight.shape[1] // hn
    half = dec_width // 2
    steps = max(zn // 2, 1)
    finish_copies = 6 + 2 * 2 * (zn - 1) + 3 * (hn - 1) + 2
    return pl.pallas_call(
        functools.partial(finish, zn, hn),
        out_shape=(
            jax.ShapeDtypeStruct(patch_hidden.shape, BF16),
            jax.ShapeDtypeStruct((bytes_, out_width), BF16),
        ),
        in_specs=[in_vmem(), in_vmem(), in_place(), in_place()] + [in_vmem()] * 8,
        out_specs=(in_vmem(), in_vmem()),
        scratch_shapes=[
            VMEM((heads * dim, out_weight.shape[2]), BF16),
            VMEM((kv_rows, 2 * dec_width), BF16),
            VMEM((heads // 2, 2, steps, dim + 16, tile), BF16),
            VMEM((heads // 2, 2, steps, dim + 16, tile), BF16),
            VMEM((heads // 2, dim + 16, 2 * new), BF16),
            VMEM((heads // 2, dim + 16, tile), BF16),
            VMEM((heads * dim, 2 * new), BF16),
            VMEM((2 * new, heads * dim), BF16),
            VMEM((max(hn - 1, 1), new, slice_width), BF16),
            VMEM((max(hn - 1, 1), new, slice_width), BF16),
            VMEM((hn, new, slice_width), BF16),
            VMEM((2, new, dec_width), BF16),
            VMEM((total, dec_width), BF16),
            VMEM((2, bytes_, dec_width), BF16),
            VMEM((2 * bytes_, dec_width), BF16),
            VMEM((2, 1, bytes_), jnp.int32),
            VMEM((half, 2 * bytes_), BF16),
            VMEM((dec_width, bytes_), BF16),
            VMEM((max(hn - 1, 1), bytes_, out_width), BF16),
            VMEM((max(hn - 1, 1), bytes_, out_width), BF16),
            pltpu.SemaphoreType.DMA((finish_copies,)),
            pltpu.SemaphoreType.DMA((finish_copies,)),
            pltpu.SemaphoreType.DMA((2,)),
        ],
        compiler_params=pltpu.CompilerParams(
            collective_id=1, has_side_effects=True, vmem_limit_bytes=48 * 2**20
        ),
        name="finish",
    )(
        partial,
        patch_hidden,
        out_weight.reshape(heads * dim, -1),
        dec_kv_weight.reshape(kv_rows, 2 * dec_width),
        norm_gain.reshape(hn, slice_width),
        jnp.concatenate([key_gain, key_gain]).reshape(1, dec_width),
        jnp.concatenate([query_gain, query_gain]).reshape(1, dec_width),
        dec_query_weight,
        dec_out_weight,
        byte_states,
        byte_patch.reshape(1, bytes_),
        mates,
    )


def solution(mesh):
    placed = (
        P("ctx", "head"),
        P("ctx", "head", None),
        P("ctx", "head", None),
        P("ctx", "head", None),
        P("ctx", "head", None),
        P("ctx", "head", None),
        P("ctx"),
        P(),
        P("head", None, None),
        P(),
        P(None, None, "head"),
        P(None, "head"),
        P(),
        P(),
        P("head", None),
        P("ctx", None),
        P("ctx"),
    )
    return jax.shard_map(
        functools.partial(per_device, mesh.shape["ctx"] // 4, mesh.shape["head"]),
        mesh=mesh,
        in_specs=placed,
        out_specs=(P("ctx", "head"), P("ctx", "head")),
        check_vma=False,
    )
```

time: 468 us -> 143 us (0.31)
  waiting for transfers between devices: 249 us -> 0 us
  Pallas kernels: 0 us -> 125 us
  blocking collectives: 62.4 us -> 0 us
  matrix products: 52.9 us -> 0 us
  local copies, waits for them, and re-layouts: 37.3 us -> 8.64 us
  starting transfers between devices: 20.8 us -> 0 us
  other arithmetic: 26 us -> 7.32 us
  between operations: 18.3 us -> 0.8 us
    pallas_call x0 -> x3, Pallas kernels: none -> 125 us  [the longest x1 75.9 us: per_device(): pl.pallas_call(functools.partial(finish, zn, hn), out_shape=(jax.ShapeDty...]
    reduce_scatter x1 -> x0, waiting for transfers between devices: 118 us -> none  [side_by_side(): lax.psum_scatter(both, axis, scatter_dimension=dim, tiled=True)]
    all_gather x1 -> x0, waiting for transfers between devices: 67.7 us -> none  [sent_together(): lax.all_gather(both, axis, axis=dim, tiled=True)]
    all_to_all x3 -> x0, waiting for transfers between devices: 63.5 us -> none  [the longest x2 47.7 us: sent_to_all(): return lax.all_to_all(copies, axis, split_axis=0, concat_axis=0, tiled=True)]
    all_to_all x3 -> x0, blocking collectives: 62.4 us -> none  [the longest x2 43.7 us: sent_to_all(): return lax.all_to_all(copies, axis, split_axis=0, concat_axis=0, tiled=True)]
    dot_general x14 -> x0, matrix products: 52.9 us -> none  [the longest x4 29.6 us: one_head(): jnp.dot(weights.astype(jnp.bfloat16), value_head, preferred_element_type=...]
    all_to_all x3 -> x0, starting transfers between devices: 20.7 us -> none  [the longest x2 14.6 us: sent_to_all(): return lax.all_to_all(copies, axis, split_axis=0, concat_axis=0, tiled=True)]
    reduce_sum x10 -> x0, other arithmetic: 12.6 us -> none  [the longest x4 11.8 us: one_head(): return (mixed_rows, jnp.sum(weights, axis=1), highest)]
  transfers between devices with their start and end apart: 5 -> 0, of which waited for: 5 -> 0; matrix products, arithmetic and copies ran while one was open for 3% -> 0% of each run, Pallas kernels for 0% -> 0%
where the time goes in v1:
time: 143 us; the launch traced here: 142 us
  Pallas kernels  125 us (87%)
  local copies, waits for them, and re-layouts  8.64 us (6%)
  other arithmetic  7.32 us (5%)
    pallas_call x1, Pallas kernels, per_device(): pl.pallas_call(functools.partial(finish, zn, hn), out_shape=(jax.ShapeDty...  75.9 us
    pallas_call x1, Pallas kernels, per_device(): pl.pallas_call(functools.partial(attend, 2 * cached, block, dim ** (-0.5)...  25.2 us
    pallas_call x1, Pallas kernels, per_device(): pl.pallas_call(functools.partial(spread, zn), out_shape=(jax.ShapeDtypeSt...  24.2 us
    unnamed x36, local copies, waits for them, and re-layouts  7.46 us
    concatenate x1, other arithmetic, per_device(): jnp.concatenate([cache_keys, new_keys], 0)  3.98 us

profile of v1, /device:TPU:1, one launch (start us, length us, event | category | flops | bytes accessed | tf_op | source)
XLA Modules:
  0.0 142.0 jit_solution(10046246689854057924)
XLA Ops:
  0.7 2.8 %pad_maximum_fusion.1 = bf16[1088,4,128]{2,1,0:T(4,128)(2,1)S(1)} fusion(bf16[64,4,128]{2,1,0:T(4,128)(2,1)} %param.20, bf16[1024,4,128]{2,1,0:T(4,128)(2,1)} %param.22), kind=kLoop, calls=%fused_computation.4 | loop fusion | flops 557056 | bytes 2228224 | tf_op jit(solution)/shard_map/concatenate | solution.py:510
  3.4 4.0 %pad_maximum_fusion = bf16[1088,4,128]{2,1,0:T(4,128)(2,1)S(1)} fusion(bf16[64,4,128]{2,1,0:T(4,128)(2,1)S(1)} %copy-done.12, bf16[1024,4,128]{2,1,0:T(4,128)(2,1)S(1)} %copy-done.11), kind=kLoop, calls=%fused_computation.3 | loop fusion | flops 557056 | bytes 2228224 | tf_op jit(solution)/shard_map/concatenate | solution.py:509
  7.4 0.0 copy-start.13
  7.4 0.0 copy-start.4
  7.4 0.0 copy-start.6
  7.5 0.4 copy_bitcast_fusion.1
  7.9 0.4 copy-done.13
  8.3 24.2 %spread.1 = (bf16[2048,256]{1,0:T(8,128)(2,1)S(1)}, bf16[2176,256]{1,0:T(8,128)(2,1)S(1)}, bf16[2176,256]{1,0:T(8,128)(2,1)S(1)}, s32[8,2048]{1,0:T(8,128)S(1)}) custom-call(bf16[64,512]{1,0:T(8,128)(2,1)S(1)} %bitcast.23, bf16[1088,512]{1,0:T(8,128)(2,1)S(1)} %get-tuple-element.11.k_ref, bf16[1088,512]{1,0:T(8,128)(2,1)S(1)} %get-tuple-element.10.v_ref, ...), custom_call_target="tpu_custom_call" | custom-call | tf_op jit(solution)/shard_map/spread/pallas_call | solution.py:514
  32.5 0.0 copy-start.14
  32.5 0.0 copy-start.10
  32.5 25.2 %attend.1.part = bf16[8,2,144,256]{3,2,1,0:T(8,128)(2,1)S(1)} custom-call(bf16[2048,256]{1,0:T(8,128)(2,1)S(1)} %get-tuple-element.6.q_ref, bf16[2176,256]{1,0:T(8,128)(2,1)S(1)} %get-tuple-element.7.k_ref, bf16[2176,256]{1,0:T(8,128)(2,1)S(1)} %get-tuple-element.8.v_ref, s32[8,2048]{1,0:T(8,128)S(1)} %get-tuple-element.9.bv_ref.bs_ref, ...), custom_call_target="tpu_custom_call" | custom-call | tf_op jit(solution)/shard_map/attend/pallas_call | solution.py:538
  57.8 0.6 maximum_bitcast_fusion
  58.4 0.3 copy.27
  58.7 0.7 reshape.44.gain_ref
  59.4 1.0 copy-done
  60.4 0.9 copy-done.2
  61.4 0.8 copy-done.3
  62.2 0.7 copy-done.5
  62.9 0.7 copy-done.7
  63.6 0.7 copy-done.8
  64.2 0.7 copy-done.9
  64.9 75.9 %finish.1 = (bf16[64,512]{1,0:T(8,128)(2,1)S(1)}, bf16[256,128]{1,0:T(8,128)(2,1)S(1)}) custom-call(bf16[8,2,144,256]{3,2,1,0:T(8,128)(2,1)S(1)} %attend.1.part, bf16[64,512]{1,0:T(8,128)(2,1)S(1)} %copy-done.3, bf16[512,4096]{1,0:T(8,128)(2,1)} %bitcast.30, bf16[4096,256]{1,0:T(8,128)(2,1)S(1)} %bitcast.22, f32[8,512]{1,0:T(8,128)S(1)} %reshape.44.gain_ref, ...), custom_call_target="tpu_custom_call" | custom-call | tf_op jit(solution)/shard_map/finish/pallas_call | solution.py:566
  140.8 0.6 copy.31
  141.4 0.6 copy.32
  (20 shorter events, 0.0 us)
Async XLA Ops:
  0.6 2.8 %copy-start.12 = (bf16[64,4,128]{2,1,0:T(4,128)(2,1)S(1)}, bf16[64,4,128]{2,1,0:T(4,128)(2,1)}, u32[]{:S(2)}) copy-start(bf16[64,4,128]{2,1,0:T(4,128)(2,1)} %param.19) | copy-start | bytes 196612
  0.6 2.8 %copy-start.11 = (bf16[1024,4,128]{2,1,0:T(4,128)(2,1)S(1)}, bf16[1024,4,128]{2,1,0:T(4,128)(2,1)}, u32[]{:S(2)}) copy-start(bf16[1024,4,128]{2,1,0:T(4,128)(2,1)} %param.21) | copy-start | bytes 3145732
  7.4 0.8 copy-start.13
  7.4 0.8 copy-start.4
  7.4 0.8 copy-start.6
  32.5 25.3 %copy-start.14 = (f32[64]{0:T(128)S(1)}, f32[64]{0:T(128)}, u32[]{:S(2)}) copy-start(f32[64]{0:T(128)} %param.30) | copy-start | bytes 772
  32.5 25.3 %copy-start.15 = (f32[64]{0:T(128)S(1)}, f32[64]{0:T(128)}, u32[]{:S(2)}) copy-start(f32[64]{0:T(128)} %param.29) | copy-start | bytes 772
  32.5 25.9 %copy-start.10 = (bf16[4096,2,128]{2,1,0:T(2,128)(2,1)S(1)}, bf16[4096,2,128]{2,1,0:T(2,128)(2,1)}, u32[]{:S(2)}) copy-start(bf16[4096,2,128]{2,1,0:T(2,128)(2,1)} %param.27) | copy-start | bytes 6291460
  58.4 1.0 copy-start.1
  59.4 1.0 copy-start
  60.4 0.9 copy-start.2
  61.4 0.8 copy-start.3
  62.2 0.7 copy-start.5
  62.9 0.7 copy-start.7
  63.6 0.7 copy-start.8
  64.2 0.7 copy-start.9

commit v2 on v1

v2 whole, which is shorter than its diff:
```python
import functools

import jax
import jax.numpy as jnp
from jax import lax
from jax.experimental import pallas as pl
from jax.experimental.pallas import tpu as pltpu
from jax.sharding import PartitionSpec as P

MESH = pl.DeviceIdType.MESH
VMEM = pltpu.VMEM
F32 = jnp.float32
BF16 = jnp.bfloat16
LOW = -1e20
HIDE = -1e30
LOG2E = 1.4426950408889634


def in_vmem():
    return pl.BlockSpec(memory_space=pltpu.VMEM)


def in_place():
    return pl.BlockSpec(memory_space=pl.ANY)


class Place:
    def __init__(self, zn):
        c = lax.axis_index("ctx")
        self.c = c
        self.zn = zn
        self.z = lax.div(c, 4)
        self.yl = lax.rem(lax.div(c, 2), 2)
        self.k = lax.rem(c, 2)
        self.cores = (self.k, 1 - self.k)

    def around(self, step):
        return lax.rem(self.z + (step + 2 * self.zn), self.zn)

    def device(self, step, other_y, other_core):
        y = 1 - self.yl if other_y else self.yl
        return {"ctx": self.around(step) * 4 + y * 2 + self.cores[other_core]}

    def near(self):
        found = [self.device(0, False, True)]
        for core in (False, True):
            found.append(self.device(0, True, core))
            found += [self.device(way, False, core) for way in (1, -1)]
        return found


class Copy:
    def __init__(self, dma):
        self.dma, self.got = dma, False

    def start(self):
        self.dma.start()
        return self

    def receive(self):
        if not self.got:
            self.dma.wait_recv()
        self.got = True


class Sends:
    def __init__(self, send_sem, recv_sem):
        self.send_sem, self.recv_sem, self.made = send_sem, recv_sem, []

    def make(self, src, dst, device):
        at = len(self.made)
        copy = Copy(
            pltpu.make_async_remote_copy(
                src_ref=src,
                dst_ref=dst,
                send_sem=self.send_sem.at[at],
                recv_sem=self.recv_sem.at[at],
                device_id=device,
                device_id_type=MESH,
            )
        )
        self.made.append(copy)
        return copy.start()

    def close(self):
        for copy in self.made:
            copy.receive()
        for copy in self.made:
            copy.dma.wait_send()


class Loads:
    def __init__(self, sem):
        self.sem, self.used = sem, 0

    def start(self, src, dst):
        copy = pltpu.make_async_copy(src, dst, self.sem.at[self.used])
        self.used += 1
        copy.start()
        return copy


def greet(devices):
    barrier = pltpu.get_barrier_semaphore()
    for device in devices:
        pl.semaphore_signal(barrier, inc=1, device_id=device, device_id_type=MESH)
    pl.semaphore_wait(barrier, len(devices))


def aligned(start, size):
    return pl.ds(pl.multiple_of(start, size), size)


def ring_gather(sends, place, source, buffer, idle=()):
    zn = place.zn
    rows = source.shape[1]
    far, near = zn // 2, zn - 1 - zn // 2
    mine = buffer.at[aligned(place.c * rows, rows), :]

    def first_hop(step, other_y, cores):
        return [
            sends.make(source.at[place.cores[core]], mine, place.device(step, other_y, core)) for core in cores
        ]

    arrived = {}
    for way, count in ((1, far), (-1, near)):
        if count:
            arrived[0, way, 0] = first_hop(way, False, (0, 1))
    from_y = first_hop(0, True, (0, 1))
    first_hop(0, False, (1,))
    buffer[aligned(place.c * rows, rows), :] = source[place.k]
    for turn in range(max(far, near)):
        for stream, step in ((0, turn + 1), (1, turn)):
            y = place.yl if stream == 0 else 1 - place.yl
            counts = (far, near) if stream == 0 else (near, far)
            for way, count in zip((1, -1), counts):
                if step >= count:
                    continue
                for copy in arrived[stream, way, step - 1] if step else from_y:
                    copy.receive()
                chip = place.around(-way * step) * 2 + y
                piece = buffer.at[aligned(chip * 2 * rows, 2 * rows), :]
                arrived[stream, way, step] = [sends.make(piece, piece, place.device(way, False, 0))]
        if turn < len(idle):
            idle[turn]()
    for work in idle[max(far, near) :]:
        work()


def spread(
    zn, q_hbm, nk_hbm, nv_hbm, ck_hbm, cv_hbm, cr_hbm, nr_hbm,
    qg, kc, vc, bounds,
    q_in, new_in, old_in, nr, held, q_half, kv_half, send_sem, recv_sem, local_sem,
):
    place = Place(zn)
    sends, loads = Sends(send_sem, recv_sem), Loads(local_sem)
    k = place.k
    new, cached = nk_hbm.shape[0], ck_hbm.shape[0]
    width = q_half.shape[2]
    peer = place.device(0, False, True)
    q_load = loads.start(q_hbm, q_in)
    small = [loads.start(cr_hbm, held.at[k]), loads.start(nr_hbm, nr)]
    kv_loads = [
        (loads.start(ck_hbm, old_in.at[0]), loads.start(nk_hbm, new_in.at[0])),
        (loads.start(cv_hbm, old_in.at[1]), loads.start(nv_hbm, new_in.at[1])),
    ]
    greet(place.near())
    q_load.wait()
    flat = q_in[...].reshape(new, 2 * width)
    q_half[0] = flat[:, :width]
    q_half[1] = flat[:, width:]
    chip = place.z * 2 + place.yl
    waits = []

    def swap(which, out):
        for copy in kv_loads[which]:
            copy.wait()
        for value, count, at, to in (
            (old_in[which], cached, 0, k * cached),
            (new_in[which], new, cached, 2 * cached + k * new),
        ):
            flat = value.reshape(count, 2 * width)
            rows = pl.ds(at, count)
            kv_half[which, 0, rows, :] = flat[:, :width]
            kv_half[which, 1, rows, :] = flat[:, width:]
            target = out.at[aligned(to, count), :]
            sends.make(kv_half.at[which, 1 - k, rows, :], target, peer)
            waits.append(loads.start(kv_half.at[which, k, rows, :], target))

    def see():
        small[1].wait()
        swapped.receive()
        both = held[...]
        mates = nr[...]
        total = mates.shape[1]
        zero = jnp.zeros((1, total), F32)
        low, high, start = zero, zero, zero
        below = jnp.zeros((1, 1), F32)
        for r in range(8):
            ones = jnp.where(both <= r, 1.0, 0.0)
            upto = jnp.sum(jnp.sum(ones, axis=0), axis=(0, 1), keepdims=True)
            first = jnp.sum(jnp.where(mates < r, 1.0, 0.0), axis=1, keepdims=True)
            here = mates == r
            low = jnp.where(here, below, low)
            high = jnp.where(here, upto, high)
            start = jnp.where(here, first, start)
            below = upto
        shift = chip * 2 * new
        index = lax.broadcasted_iota(jnp.int32, (1, total), 1)
        bounds[0:1, :] = low.astype(jnp.int32)
        bounds[1:2, :] = high.astype(jnp.int32)
        bounds[2:3, :] = start.astype(jnp.int32) - shift
        bounds[3:4, :] = index - (shift - 1)
        bounds[4:8, :] = jnp.zeros((4, total), jnp.int32)

    def swap_requests():
        small[0].wait()
        return sends.make(held.at[k], held.at[k], peer)

    swapped = swap_requests()
    ring_gather(
        sends, place, q_half, qg, [functools.partial(swap, 0, kc), functools.partial(swap, 1, vc), see]
    )
    for copy in waits:
        copy.wait()
    sends.close()


def attend(cached, block, scale, q_ref, k_ref, v_ref, bv_ref, bs_ref, o_ref, m_s, l_s, acc_s):
    rows = q_ref.shape[0]
    new = k_ref.shape[0] - cached
    q0 = pl.program_id(0) * rows
    last = q0 + rows - 1
    heads, dim = acc_s.shape[0], acc_s.shape[1]

    def columns(h):
        return slice(h * dim, (h + 1) * dim)

    def scores_of(first, count, base, low, high):
        found = []
        for h in range(heads):
            scores = lax.dot_general(
                k_ref[pl.ds(first, count), columns(h)],
                q_ref[:, columns(h)],
                (((1,), (1,)), ((), ())),
                preferred_element_type=F32,
            )
            if low is not None:
                at = lax.broadcasted_iota(jnp.int32, scores.shape, 0) + base
                scores = jnp.where((at >= low) & (at < high), scores, HIDE)
            found.append(scores)
        return found

    def mixed(h, first, weights):
        return lax.dot_general(
            v_ref[pl.ds(first, weights.shape[0]), columns(h)],
            weights.astype(BF16),
            (((0,), (0,)), ((), ())),
            preferred_element_type=F32,
        )

    def top_of(scores):
        return (jnp.max(scores, axis=0, keepdims=True) * scale).astype(BF16).astype(F32)

    low_first, low_last = bs_ref[0, q0], bs_ref[0, last]
    high_first, high_last = bs_ref[1, q0], bs_ref[1, last]
    sees_new = (bs_ref[3, last] > 0) & (bs_ref[2, q0] < new)
    sees_all = (low_last <= 0) & (high_first >= cached)

    @pl.when(sees_all)
    def _():
        old = scores_of(0, cached, 0, None, None)
        late = scores_of(cached, new, 0, bv_ref[2:3, :], bv_ref[3:4, :])
        kept = []
        for h in range(heads):
            top = jnp.maximum(top_of(old[h]), top_of(late[h]))
            kept.append((jnp.exp2(old[h] * scale - top), jnp.exp2(late[h] * scale - top)))
            m_s[h] = top
        for h in range(heads):
            w_old, w_late = kept[h]
            l_s[h] = jnp.sum(w_old, axis=0, keepdims=True) + jnp.sum(w_late, axis=0, keepdims=True)
            acc_s[h] = mixed(h, 0, w_old) + mixed(h, cached, w_late)

    @pl.when(jnp.logical_not(sees_all))
    def _():
        m_s[...] = jnp.full_like(m_s, LOW).astype(BF16).astype(F32)
        l_s[...] = jnp.zeros_like(l_s)
        acc_s[...] = jnp.zeros_like(acc_s)

        def add(first, count, base, low, high):
            scores = scores_of(first, count, base, low, high)
            kept = []
            for h in range(heads):
                m_old = m_s[h]
                m_new = jnp.maximum(m_old, top_of(scores[h]))
                weights = jnp.exp2(scores[h] * scale - m_new)
                fade = jnp.exp2(m_old - m_new)
                m_s[h] = m_new
                l_s[h] = l_s[h] * fade + jnp.sum(weights, axis=0, keepdims=True)
                kept.append((fade, weights))
            for h in range(heads):
                fade, weights = kept[h]
                acc_s[h] = acc_s[h] * fade + mixed(h, first, weights)

        begin = lax.div(low_first, block)
        end = jnp.where(high_last > low_first, lax.div(high_last + block - 1, block), begin)

        def one_block(b, carry):
            first = pl.multiple_of(b * block, block)
            whole = (low_last <= first) & (high_first >= first + block)

            @pl.when(whole)
            def _():
                add(first, block, first, None, None)

            @pl.when(jnp.logical_not(whole))
            def _():
                add(first, block, first, bv_ref[0:1, :], bv_ref[1:2, :])

            return carry

        lax.fori_loop(begin, end, one_block, 0)

        @pl.when(sees_new)
        def _():
            add(cached, new, 0, bv_ref[2:3, :], bv_ref[3:4, :])

    for h in range(heads):
        pack(o_ref.at[0, h], acc_s[h], m_s[h], l_s[h])


def pack(ref, out, top, total):
    dim = out.shape[0]
    ref[0:dim, :] = out.astype(BF16)
    coarse = total.astype(BF16).astype(F32)
    row = lax.broadcasted_iota(jnp.int32, (16, out.shape[1]), 0)
    tail = jnp.where(row == 0, top, jnp.where(row == 1, coarse, jnp.where(row == 2, total - coarse, 0.0)))
    ref[dim : dim + 16, :] = tail.astype(BF16)


def unpack(ref):
    value = ref[...]
    dim = value.shape[0] - 16
    tail = value[dim:, :].astype(F32)
    return value[:dim, :].astype(F32), tail[0:1, :], tail[1:2, :] + tail[2:3, :]


def merged(parts):
    top = parts[0][1]
    for part in parts[1:]:
        top = jnp.maximum(top, part[1])
    out, total = 0.0, 0.0
    for o, m, l in parts:
        factor = jnp.exp2(m - top)
        out = out + o * factor
        total = total + l * factor
    return out, top, total


def head_norm(values, gain, half):
    lane = lax.broadcasted_iota(jnp.int32, values.shape, 1)
    first = lane < half
    squares = values * values
    s0 = jnp.sum(jnp.where(first, squares, 0.0), axis=1, keepdims=True)
    s1 = jnp.sum(jnp.where(first, 0.0, squares), axis=1, keepdims=True)
    return values * lax.rsqrt(jnp.where(first, s0, s1) / half + 1e-6) * gain


def finish(
    zn, hn, part, hidden_hbm, w_hbm, dkv_hbm, gain_hbm, kgain_hbm, qgain_hbm, dqw_hbm, dow_hbm, states_hbm, bp_hbm, nr_hbm,
    patch_out, byte_out,
    hidden, w_ref, dkv_in, dkv, gain_ref, kgain, qgain, dqw_ref, dow_ref, states_ref, nr,
    ring_in, ring_out, last, last_in, att, rs_out, rs_in, ag_in, kv_tile, kvg, bq_tile, bq,
    bp_both, mix_tile, mix, bs_out, bs_in, send_sem, recv_sem, local_sem,
):
    place = Place(zn)
    sends, loads = Sends(send_sem, recv_sem), Loads(local_sem)
    k, z, yl = place.k, place.z, place.yl
    me = lax.axis_index("head")
    peer = place.device(0, False, True)
    others = [lax.rem(me + i, hn) for i in range(1, hn)]
    sources = [me] + [lax.rem(me + hn - i, hn) for i in range(1, hn)]
    for_queries = [
        loads.start(a, b)
        for a, b in ((states_hbm, states_ref), (dqw_hbm, dqw_ref), (qgain_hbm, qgain), (bp_hbm, bp_both.at[k]))
    ]
    dkv_load = loads.start(dkv_hbm, dkv_in)
    w_loads = [loads.start(w_hbm, w_ref), loads.start(hidden_hbm, hidden)]
    late = [
        loads.start(a, b)
        for a, b in ((gain_hbm, gain_ref), (kgain_hbm, kgain), (nr_hbm, nr), (dow_hbm, dow_ref))
    ]
    greet(place.near() + [{"head": d} for d in others])
    new, slice_width = hidden.shape
    heads = part.shape[1]
    dim = part.shape[2] - 16
    bytes_, half = states_ref.shape[0], kgain.shape[1]

    swapped = []

    def byte_queries():
        for copy in for_queries:
            copy.wait()
        proj = jnp.dot(states_ref[...], dqw_ref[...], preferred_element_type=F32)
        gain = jnp.concatenate([qgain[...], qgain[...]], axis=1)
        normed = head_norm(proj, gain, half)
        lane = lax.broadcasted_iota(jnp.int32, normed.shape, 1)
        bq_tile[0] = jnp.where(lane < half, normed, 0.0).astype(BF16)
        bq_tile[1] = jnp.where(lane < half, pltpu.roll(normed, half, 1), 0.0).astype(BF16)
        rows = aligned(k * bytes_, bytes_)
        swapped.append(sends.make(bp_both.at[k], bp_both.at[k], peer))
        sends.make(bq_tile.at[1 - k], bq.at[rows, :], peer)
        bq[rows, :] = bq_tile[k]

    def flat_weights():
        dkv_load.wait()
        count = dkv.shape[0] // 4
        for i in range(4):
            rows = slice(i * count, (i + 1) * count)
            dkv[rows, :] = dkv_in[rows].reshape(count, dkv.shape[1])

    idle = [byte_queries, flat_weights]
    far, near = zn // 2, zn - 1 - zn // 2
    counts = [(far, near) if h % 2 == 0 else (near, far) for h in range(heads)]
    made = {}
    for step in range(max(far, near)):
        for h in range(heads):
            for way in (0, 1):
                count = counts[h][way]
                if step >= count:
                    continue
                sign = 1 - 2 * way
                target = place.around(sign * (count - step))
                if step == 0:
                    src = part.at[target, h]
                else:
                    made[h, way, step - 1].receive()
                    src = ring_out.at[h, way, step]
                    pack(src, *merged([unpack(part.at[target, h]), unpack(ring_in.at[h, way, step - 1])]))
                made[h, way, step] = sends.make(src, ring_in.at[h, way, step], place.device(sign, False, 0))
        if step < len(idle):
            idle[step]()
    for work in idle[max(far, near) :]:
        work()
    summed = []
    for h in range(heads):
        got = [unpack(part.at[z, h])]
        for way in (0, 1):
            count = counts[h][way]
            if count:
                made[h, way, count - 1].receive()
                got.append(unpack(ring_in.at[h, way, count - 1]))
        summed.append(merged(got))
    for y in (0, 1):
        cols = slice(y * 2 * new, (y + 1) * 2 * new)
        for core in (0, 1):
            joined = []
            for a, b in zip(*summed):
                a, b = a[:, cols], b[:, cols]
                lane = lax.broadcasted_iota(jnp.int32, a.shape, 1)
                if core == 0:
                    joined.append(jnp.where(lane < new, a, pltpu.roll(b, new, 1)))
                else:
                    joined.append(jnp.where(lane < new, pltpu.roll(a, new, 1), b))
            pack(last.at[y, core], *joined)
    across = sends.make(last.at[1 - yl, k], last_in.at[0], place.device(0, True, False))
    beside = sends.make(last.at[yl, 1 - k], last_in.at[1], peer)
    diagonal = sends.make(last.at[1 - yl, 1 - k], last_in.at[2], place.device(0, True, True))
    for pair, parts, waits in (
        (k, (last.at[yl, k], last_in.at[0]), (across,)),
        (1 - k, (last_in.at[1], last_in.at[2]), (beside, diagonal)),
    ):
        for copy in waits:
            copy.receive()
        out, _, total = merged([unpack(ref) for ref in parts])
        turned = (out / total).T.astype(BF16)
        both = jnp.concatenate([turned[:new], turned[new:]], axis=1)
        att[:, aligned(pair * 2 * dim, 2 * dim)] = both

    for copy in w_loads:
        copy.wait()
    mine = att[...]

    def columns_for(d):
        return jnp.dot(mine, w_ref[:, aligned(d * slice_width, slice_width)], preferred_element_type=F32)

    rs_sends = []
    for i, d in enumerate(others):
        rs_out[i] = columns_for(d).astype(BF16)
        rs_sends.append(sends.make(rs_out.at[i], rs_in.at[i], {"head": d}))
    own = columns_for(me) + hidden[...].astype(F32)
    for i, copy in enumerate(rs_sends):
        copy.receive()
        own = own + rs_in[i].astype(F32)
    rounded = own.astype(BF16)
    ag_in[0] = rounded
    ag_sends = [sends.make(ag_in.at[0], ag_in.at[1 + i], {"head": d}) for i, d in enumerate(others)]
    patch_out[...] = rounded
    for copy in late:
        copy.wait()
    squares, proj = 0.0, 0.0
    for i, source in enumerate(sources):
        if i:
            ag_sends[i - 1].receive()
        wide = ag_in[i].astype(F32)
        squares = squares + jnp.sum(wide * wide, axis=1, keepdims=True)
        scaled = (wide * gain_ref[:, aligned(source * slice_width, slice_width)]).astype(BF16)
        rows = aligned(source * slice_width, slice_width)
        proj = proj + jnp.dot(scaled, dkv[rows, :], preferred_element_type=F32)
    proj = proj * lax.rsqrt(squares / (hn * slice_width) + 1e-5)
    width = 2 * half
    keys = head_norm(proj[:, :width], jnp.concatenate([kgain[...], kgain[...]], axis=1), half)
    values = proj[:, width:]
    lane = lax.broadcasted_iota(jnp.int32, keys.shape, 1)
    kv_tile[0] = jnp.where(lane < half, keys, pltpu.roll(values, half, 1)).astype(BF16)
    kv_tile[1] = jnp.where(lane < half, pltpu.roll(keys, half, 1), values).astype(BF16)

    spans = []

    def byte_spans():
        swapped[0].receive()
        owner = jnp.concatenate([bp_both[0], bp_both[1]], axis=1)
        first = jnp.zeros(owner.shape, F32)
        mates = nr[...]
        for r in range(1, 8):
            begins = jnp.sum(jnp.where(mates < r, 1.0, 0.0), axis=1, keepdims=True)
            first = jnp.where(owner.astype(F32) >= begins, begins, first)
        spans.append((first.astype(jnp.int32), owner))

    ring_gather(sends, place, kv_tile, kvg, [byte_spans])
    for copy in sends.made:
        copy.receive()
    first, owner = spans[0]

    queries = bq[...]
    block = min(512, kvg.shape[0])
    scale = half ** (-0.5) * LOG2E
    out, total = 0.0, 0.0
    for b in range(kvg.shape[0] // block):
        kv = kvg[b * block : (b + 1) * block, :]
        scores = lax.dot_general(kv, queries, (((1,), (1,)), ((), ())), preferred_element_type=F32)
        at = lax.broadcasted_iota(jnp.int32, scores.shape, 0) + b * block
        weights = jnp.where((at >= first) & (at <= owner), jnp.exp2(scores * scale), 0.0)
        total = total + jnp.sum(weights, axis=0, keepdims=True)
        out = out + lax.dot_general(
            kv, weights.astype(BF16), (((0,), (0,)), ((), ())), preferred_element_type=F32
        )
    mix_tile[...] = (out[half:, :] / total).astype(BF16)
    mix_rows = aligned(k * half, half)
    theirs, ours = aligned((1 - k) * bytes_, bytes_), aligned(k * bytes_, bytes_)
    mix_send = sends.make(mix_tile.at[:, theirs], mix.at[mix_rows, :], peer)
    mix[mix_rows, :] = mix_tile[:, ours]
    mix_send.receive()
    mixed = mix[...]
    out_width = byte_out.shape[1]

    def byte_columns_for(d):
        cols = aligned(d * out_width, out_width)
        return lax.dot_general(mixed, dow_ref[:, cols], (((0,), (0,)), ((), ())), preferred_element_type=F32)

    bs_sends = []
    for i, d in enumerate(others):
        bs_out[i] = byte_columns_for(d).astype(BF16)
        bs_sends.append(sends.make(bs_out.at[i], bs_in.at[i], {"head": d}))
    own = byte_columns_for(me) + states_ref[:, aligned(me * out_width, out_width)].astype(F32)
    for i, copy in enumerate(bs_sends):
        copy.receive()
        own = own + bs_in[i].astype(F32)
    byte_out[...] = own.astype(BF16)
    sends.close()


def per_device(
    zn,
    hn,
    patch_hidden,
    queries,
    new_keys,
    new_values,
    cache_keys,
    cache_values,
    cache_request,
    new_request,
    out_weight,
    norm_gain,
    dec_kv_weight,
    dec_query_weight,
    query_gain,
    key_gain,
    dec_out_weight,
    byte_states,
    byte_patch,
):
    new, heads, dim = queries.shape
    cached = cache_keys.shape[0]
    total = new_request.shape[0]
    pair = heads // 2 * dim
    all_keys = 2 * (cached + new)
    slice_width = patch_hidden.shape[1]
    held = cache_request.reshape(8, cached // 8)
    mates = new_request.reshape(1, total)
    gather_copies = 1 + 4 + 7 + 2 * zn
    gathered, keys, values, bounds = pl.pallas_call(
        functools.partial(spread, zn),
        out_shape=(
            jax.ShapeDtypeStruct((total, pair), BF16),
            jax.ShapeDtypeStruct((all_keys, pair), BF16),
            jax.ShapeDtypeStruct((all_keys, pair), BF16),
            jax.ShapeDtypeStruct((8, total), jnp.int32),
        ),
        in_specs=[in_place()] * 7,
        out_specs=(in_vmem(),) * 4,
        scratch_shapes=[
            VMEM(queries.shape, BF16),
            VMEM((2, *new_keys.shape), BF16),
            VMEM((2, *cache_keys.shape), BF16),
            VMEM((1, total), jnp.int32),
            VMEM((2, *held.shape), jnp.int32),
            VMEM((2, new, pair), BF16),
            VMEM((2, 2, cached + new, pair), BF16),
            pltpu.SemaphoreType.DMA((gather_copies,)),
            pltpu.SemaphoreType.DMA((gather_copies,)),
            pltpu.SemaphoreType.DMA((11,)),
        ],
        compiler_params=pltpu.CompilerParams(
            collective_id=0, has_side_effects=True, vmem_limit_bytes=32 * 2**20
        ),
        name="spread",
    )(queries, new_keys, new_values, cache_keys, cache_values, held, mates)

    tile = 4 * new
    block = min(512, cached)
    partial = pl.pallas_call(
        functools.partial(attend, 2 * cached, block, dim ** (-0.5) * LOG2E),
        out_shape=jax.ShapeDtypeStruct((zn, heads // 2, dim + 16, tile), BF16),
        grid=(zn,),
        in_specs=[
            pl.BlockSpec((tile, pair), lambda t: (t, 0)),
            pl.BlockSpec((all_keys, pair), lambda t: (0, 0)),
            pl.BlockSpec((all_keys, pair), lambda t: (0, 0)),
            pl.BlockSpec((8, tile), lambda t: (0, t)),
            pl.BlockSpec(memory_space=pltpu.SMEM),
        ],
        out_specs=pl.BlockSpec((1, heads // 2, dim + 16, tile), lambda t: (t, 0, 0, 0)),
        scratch_shapes=[
            VMEM((heads // 2, 1, tile), F32),
            VMEM((heads // 2, 1, tile), F32),
            VMEM((heads // 2, dim, tile), F32),
        ],
        compiler_params=pltpu.CompilerParams(vmem_limit_bytes=40 * 2**20),
        name="attend",
    )(gathered, keys, values, bounds, bounds)

    kv_rows = dec_kv_weight.shape[0]
    dec_width = dec_kv_weight.shape[2]
    bytes_ = byte_states.shape[0]
    out_width = dec_out_weight.shape[1] // hn
    half = dec_width // 2
    steps = max(zn // 2, 1)
    peers = max(hn - 1, 1)
    finish_copies = 2 + 2 * (zn - 1) + 3 + 3 * (hn - 1) + 7 + 2 * zn + 1
    flat_weight = out_weight.reshape(heads * dim, -1)
    return pl.pallas_call(
        functools.partial(finish, zn, hn),
        out_shape=(
            jax.ShapeDtypeStruct(patch_hidden.shape, BF16),
            jax.ShapeDtypeStruct((bytes_, out_width), BF16),
        ),
        in_specs=[in_vmem()] + [in_place()] * 11,
        out_specs=(in_vmem(), in_vmem()),
        scratch_shapes=[
            VMEM(patch_hidden.shape, BF16),
            VMEM(flat_weight.shape, BF16),
            VMEM(dec_kv_weight.shape, BF16),
            VMEM((kv_rows, 2 * dec_width), BF16),
            VMEM((1, kv_rows), F32),
            VMEM((1, half), F32),
            VMEM((1, half), F32),
            VMEM(dec_query_weight.shape, BF16),
            VMEM(dec_out_weight.shape, BF16),
            VMEM(byte_states.shape, BF16),
            VMEM((1, total), jnp.int32),
            VMEM((heads // 2, 2, steps, dim + 16, tile), BF16),
            VMEM((heads // 2, 2, steps, dim + 16, tile), BF16),
            VMEM((2, 2, dim + 16, 2 * new), BF16),
            VMEM((3, dim + 16, 2 * new), BF16),
            VMEM((new, heads * dim), BF16),
            VMEM((peers, new, slice_width), BF16),
            VMEM((peers, new, slice_width), BF16),
            VMEM((hn, new, slice_width), BF16),
            VMEM((2, new, dec_width), BF16),
            VMEM((total, dec_width), BF16),
            VMEM((2, bytes_, dec_width), BF16),
            VMEM((2 * bytes_, dec_width), BF16),
            VMEM((2, 1, bytes_), jnp.int32),
            VMEM((half, 2 * bytes_), BF16),
            VMEM((dec_width, bytes_), BF16),
            VMEM((peers, bytes_, out_width), BF16),
            VMEM((peers, bytes_, out_width), BF16),
            pltpu.SemaphoreType.DMA((finish_copies,)),
            pltpu.SemaphoreType.DMA((finish_copies,)),
            pltpu.SemaphoreType.DMA((11,)),
        ],
        compiler_params=pltpu.CompilerParams(
            collective_id=1, has_side_effects=True, vmem_limit_bytes=48 * 2**20
        ),
        name="finish",
    )(
        partial,
        patch_hidden,
        flat_weight,
        dec_kv_weight,
        norm_gain.reshape(1, kv_rows),
        key_gain.reshape(1, half),
        query_gain.reshape(1, half),
        dec_query_weight,
        dec_out_weight,
        byte_states,
        byte_patch.reshape(1, bytes_),
        mates,
    )


def solution(mesh):
    placed = (
        P("ctx", "head"),
        P("ctx", "head", None),
        P("ctx", "head", None),
        P("ctx", "head", None),
        P("ctx", "head", None),
        P("ctx", "head", None),
        P("ctx"),
        P(),
        P("head", None, None),
        P(),
        P(None, None, "head"),
        P(None, "head"),
        P(),
        P(),
        P("head", None),
        P("ctx", None),
        P("ctx"),
    )
    return jax.shard_map(
        functools.partial(per_device, mesh.shape["ctx"] // 4, mesh.shape["head"]),
        mesh=mesh,
        in_specs=placed,
        out_specs=(P("ctx", "head"), P("ctx", "head")),
        check_vma=False,
    )
```

time: 143 us -> 125 us (0.87)
  Pallas kernels: 125 us -> 116 us
  other arithmetic: 7.32 us -> 0 us
    pallas_call x1, Pallas kernels: 25.2 us -> 14.9 us  [per_device(): pl.pallas_call(functools.partial(attend, 2 * cached, block, dim ** (-0.5)...]
    concatenate x2 -> x0, other arithmetic: 6.74 us -> none  [the longest x1 3.98 us: per_device(): jnp.concatenate([cache_keys, new_keys], 0)]
where the time goes in v2:
time: 125 us
  Pallas kernels  116 us (93%)
  local copies, waits for them, and re-layouts  7.67 us (6%)
    pallas_call x1, Pallas kernels, per_device(): pl.pallas_call(functools.partial(finish, zn, hn), out_shape=(jax.ShapeDty...  76 us
    pallas_call x1, Pallas kernels, per_device(): pl.pallas_call(functools.partial(spread, zn), out_shape=(jax.ShapeDtypeSt...  25.4 us
    pallas_call x1, Pallas kernels, per_device(): pl.pallas_call(functools.partial(attend, 2 * cached, block, dim ** (-0.5)...  14.9 us
    unnamed x36, local copies, waits for them, and re-layouts  7.67 us

profile of v2, /device:TPU:1, one launch (start us, length us, event | category | flops | bytes accessed | tf_op | source)
XLA Modules:
  0.0 124.7 jit_solution(16209546032376288058)
XLA Ops:
  0.6 0.0 copy-start.1
  0.6 1.2 copy-done.1
  1.9 1.2 copy-done.2
  3.1 0.8 copy-done.7
  3.9 0.8 copy-done.8
  4.8 0.8 copy-done.9
  5.6 0.7 copy-done.10
  6.3 0.7 copy-done.13
  7.0 25.4 %spread.1 = (bf16[2048,256]{1,0:T(8,128)(2,1)S(1)}, bf16[2176,256]{1,0:T(8,128)(2,1)S(1)}, bf16[2176,256]{1,0:T(8,128)(2,1)S(1)}, s32[8,2048]{1,0:T(8,128)S(1)}) custom-call(bf16[64,4,128]{2,1,0:T(4,128)(2,1)S(1)} %copy-done.7, bf16[64,4,128]{2,1,0:T(4,128)(2,1)S(1)} %copy-done.8, bf16[64,4,128]{2,1,0:T(4,128)(2,1)S(1)} %copy-done.9, ...), custom_call_target="tpu_custom_call" | custom-call | tf_op jit(solution)/shard_map/spread/pallas_call | solution.py:603
  32.4 0.0 copy-start
  32.4 0.0 copy-start.3
  32.4 0.0 copy-start.4
  32.4 0.0 copy-start.5
  32.4 0.0 copy-start.6
  32.4 0.0 copy-start.11
  32.4 0.0 copy-start.12
  32.5 0.0 copy-start.14
  32.5 0.0 copy-start.15
  32.5 0.0 copy-start.16
  32.5 14.9 %attend.1.part = bf16[8,2,144,256]{3,2,1,0:T(8,128)(2,1)S(1)} custom-call(bf16[2048,256]{1,0:T(8,128)(2,1)S(1)} %get-tuple-element.6.q_ref, bf16[2176,256]{1,0:T(8,128)(2,1)S(1)} %get-tuple-element.7.k_ref, bf16[2176,256]{1,0:T(8,128)(2,1)S(1)} %get-tuple-element.8.v_ref, s32[8,2048]{1,0:T(8,128)S(1)} %get-tuple-element.9.bv_ref.bs_ref, ...), custom_call_target="tpu_custom_call" | custom-call | tf_op jit(solution)/shard_map/attend/pallas_call | solution.py:633
  47.4 0.0 copy-done
  47.5 76.0 %finish.1 = (bf16[64,512]{1,0:T(8,128)(2,1)S(1)}, bf16[256,128]{1,0:T(8,128)(2,1)S(1)}) custom-call(bf16[8,2,144,256]{3,2,1,0:T(8,128)(2,1)S(1)} %attend.1.part, bf16[64,512]{1,0:T(8,128)(2,1)S(1)} %copy-done.6, bf16[512,4096]{1,0:T(8,128)(2,1)} %bitcast.14, bf16[4096,2,128]{2,1,0:T(2,128)(2,1)S(1)} %copy-done, f32[1,4096]{1,0:T(1,128)S(1)} %bitcast.9, ...), custom_call_target="tpu_custom_call" | custom-call | tf_op jit(solution)/shard_map/finish/pallas_call | solution.py:663
  123.4 0.6 copy.21
  124.1 0.6 copy.22
  (15 shorter events, 0.0 us)
Async XLA Ops:
  0.6 1.2 copy-start.1
  1.9 1.2 copy-start.2
  3.1 0.8 copy-start.7
  3.9 0.8 copy-start.8
  4.8 0.8 copy-start.9
  5.6 0.7 copy-start.10
  6.3 0.7 copy-start.13
  32.4 15.0 %copy-start = (bf16[4096,2,128]{2,1,0:T(2,128)(2,1)S(1)}, bf16[4096,2,128]{2,1,0:T(2,128)(2,1)}, u32[]{:S(2)}) copy-start(bf16[4096,2,128]{2,1,0:T(2,128)(2,1)} %dkv_hbm.1) | copy-start | bytes 6291460
  32.4 15.0 %copy-start.3 = (bf16[256,1024]{1,0:T(8,128)(2,1)S(1)}, bf16[256,1024]{1,0:T(8,128)(2,1)}, u32[]{:S(2)}) copy-start(bf16[256,1024]{1,0:T(8,128)(2,1)} %states_hbm.1) | copy-start | bytes 1572868
  32.4 15.0 %copy-start.4 = (bf16[1024,128]{1,0:T(8,128)(2,1)S(1)}, bf16[1024,128]{1,0:T(8,128)(2,1)}, u32[]{:S(2)}) copy-start(bf16[1024,128]{1,0:T(8,128)(2,1)} %dqw_hbm.1) | copy-start | bytes 786436
  32.4 15.0 %copy-start.5 = (bf16[128,1024]{1,0:T(8,128)(2,1)S(1)}, bf16[128,1024]{1,0:T(8,128)(2,1)}, u32[]{:S(2)}) copy-start(bf16[128,1024]{1,0:T(8,128)(2,1)} %dow_hbm.1) | copy-start | bytes 786436
  32.4 15.0 %copy-start.6 = (bf16[64,512]{1,0:T(8,128)(2,1)S(1)}, bf16[64,512]{1,0:T(8,128)(2,1)}, u32[]{:S(2)}) copy-start(bf16[64,512]{1,0:T(8,128)(2,1)} %hidden_hbm.1) | copy-start | bytes 196612
  32.4 15.0 %copy-start.11 = (s32[2048]{0:T(1024)S(1)}, s32[2048]{0:T(1024)}, u32[]{:S(2)}) copy-start(s32[2048]{0:T(1024)} %param.24) | copy-start | bytes 24580
  32.4 15.0 %copy-start.12 = (f32[4096]{0:T(1024)S(1)}, f32[4096]{0:T(1024)}, u32[]{:S(2)}) copy-start(f32[4096]{0:T(1024)} %param.26) | copy-start | bytes 49156
  32.5 15.0 %copy-start.14 = (s32[256]{0:T(256)S(1)}, s32[256]{0:T(256)}, u32[]{:S(2)}) copy-start(s32[256]{0:T(256)} %param.33) | copy-start | bytes 3076
  32.5 15.0 %copy-start.15 = (f32[64]{0:T(128)S(1)}, f32[64]{0:T(128)}, u32[]{:S(2)}) copy-start(f32[64]{0:T(128)} %param.30) | copy-start | bytes 772
  32.5 15.0 %copy-start.16 = (f32[64]{0:T(128)S(1)}, f32[64]{0:T(128)}, u32[]{:S(2)}) copy-start(f32[64]{0:T(128)} %param.29) | copy-start | bytes 772

commit v3 on v2

--- a/solution.py
+++ b/solution.py
@@ -21,7 +21,7 @@
 
 
 def in_place():
-    return pl.BlockSpec(memory_space=pl.ANY)
+    return pl.BlockSpec(memory_space=pltpu.HBM)
 
 
 class Place:
@@ -41,11 +41,11 @@
         y = 1 - self.yl if other_y else self.yl
         return {"ctx": self.around(step) * 4 + y * 2 + self.cores[other_core]}
 
-    def near(self):
+    def near(self, steps):
         found = [self.device(0, False, True)]
         for core in (False, True):
             found.append(self.device(0, True, core))
-            found += [self.device(way, False, core) for way in (1, -1)]
+            found += [self.device(step, False, core) for step in steps]
         return found
 
 
@@ -111,40 +111,62 @@
     return pl.ds(pl.multiple_of(start, size), size)
 
 
+def first_hop(sends, place, source, buffer, step, other_y, cores):
+    rows = source.shape[1]
+    mine = buffer.at[aligned(place.c * rows, rows), :]
+    return [sends.make(source.at[place.cores[core]], mine, place.device(step, other_y, core)) for core in cores]
+
+
 def ring_gather(sends, place, source, buffer, idle=()):
     zn = place.zn
     rows = source.shape[1]
     far, near = zn // 2, zn - 1 - zn // 2
-    mine = buffer.at[aligned(place.c * rows, rows), :]
-
-    def first_hop(step, other_y, cores):
-        return [
-            sends.make(source.at[place.cores[core]], mine, place.device(step, other_y, core)) for core in cores
-        ]
-
     arrived = {}
     for way, count in ((1, far), (-1, near)):
         if count:
-            arrived[0, way, 0] = first_hop(way, False, (0, 1))
-    from_y = first_hop(0, True, (0, 1))
-    first_hop(0, False, (1,))
+            for core, copy in enumerate(first_hop(sends, place, source, buffer, way, False, (0, 1))):
+                arrived[0, core, way, 0] = copy
+    from_y = first_hop(sends, place, source, buffer, 0, True, (0, 1))
+    first_hop(sends, place, source, buffer, 0, False, (1,))
     buffer[aligned(place.c * rows, rows), :] = source[place.k]
     for turn in range(max(far, near)):
         for stream, step in ((0, turn + 1), (1, turn)):
             y = place.yl if stream == 0 else 1 - place.yl
             counts = (far, near) if stream == 0 else (near, far)
-            for way, count in zip((1, -1), counts):
-                if step >= count:
-                    continue
-                for copy in arrived[stream, way, step - 1] if step else from_y:
-                    copy.receive()
-                chip = place.around(-way * step) * 2 + y
-                piece = buffer.at[aligned(chip * 2 * rows, 2 * rows), :]
-                arrived[stream, way, step] = [sends.make(piece, piece, place.device(way, False, 0))]
+            for core in (0, 1):
+                for way, count in zip((1, -1), counts):
+                    if step >= count:
+                        continue
+                    (arrived[stream, core, way, step - 1] if step else from_y[core]).receive()
+                    owner = place.around(-way * step) * 4 + y * 2 + place.cores[core]
+                    piece = buffer.at[aligned(owner * rows, rows), :]
+                    arrived[stream, core, way, step] = sends.make(piece, piece, place.device(way, False, 0))
         if turn < len(idle):
             idle[turn]()
     for work in idle[max(far, near) :]:
         work()
+
+
+def line_steps(zn):
+    return sorted([way * n for n in range(1, zn // 2 + 1) for way in (1, -1) if 2 * n < zn or way > 0], key=lambda n: -abs(n))
+
+
+def line_gather(sends, place, source, buffer, idle=()):
+    rows = source.shape[1]
+    found = {}
+    for step in line_steps(place.zn):
+        found[step] = first_hop(sends, place, source, buffer, step, False, (0, 1))
+    found[0] = first_hop(sends, place, source, buffer, 0, False, (1,))
+    first_hop(sends, place, source, buffer, 0, True, (0, 1))
+    buffer[aligned(place.c * rows, rows), :] = source[place.k]
+    for work in idle:
+        work()
+    for step in reversed(line_steps(place.zn)):
+        for copy in found[step]:
+            copy.receive()
+        chip = place.around(-step) * 2 + place.yl
+        piece = buffer.at[aligned(chip * 2 * rows, 2 * rows), :]
+        sends.make(piece, piece, place.device(0, True, False))
 
 
 def spread(
@@ -164,7 +186,7 @@
         (loads.start(ck_hbm, old_in.at[0]), loads.start(nk_hbm, new_in.at[0])),
         (loads.start(cv_hbm, old_in.at[1]), loads.start(nv_hbm, new_in.at[1])),
     ]
-    greet(place.near())
+    greet(place.near((1, -1)))
     q_load.wait()
     flat = q_in[...].reshape(new, 2 * width)
     q_half[0] = flat[:, :width]
@@ -226,30 +248,12 @@
     sends.close()
 
 
-def attend(cached, block, scale, q_ref, k_ref, v_ref, bv_ref, bs_ref, o_ref, m_s, l_s, acc_s):
-    rows = q_ref.shape[0]
+def attend(rows, cached, block, scale, q_ref, k_ref, v_ref, bv_ref, bs_ref, o_ref, m_s, l_s, acc_s):
     new = k_ref.shape[0] - cached
-    q0 = pl.program_id(0) * rows
-    last = q0 + rows - 1
     heads, dim = acc_s.shape[0], acc_s.shape[1]
 
     def columns(h):
         return slice(h * dim, (h + 1) * dim)
-
-    def scores_of(first, count, base, low, high):
-        found = []
-        for h in range(heads):
-            scores = lax.dot_general(
-                k_ref[pl.ds(first, count), columns(h)],
-                q_ref[:, columns(h)],
-                (((1,), (1,)), ((), ())),
-                preferred_element_type=F32,
-            )
-            if low is not None:
-                at = lax.broadcasted_iota(jnp.int32, scores.shape, 0) + base
-                scores = jnp.where((at >= low) & (at < high), scores, HIDE)
-            found.append(scores)
-        return found
 
     def mixed(h, first, weights):
         return lax.dot_general(
@@ -262,71 +266,95 @@
     def top_of(scores):
         return (jnp.max(scores, axis=0, keepdims=True) * scale).astype(BF16).astype(F32)
 
-    low_first, low_last = bs_ref[0, q0], bs_ref[0, last]
-    high_first, high_last = bs_ref[1, q0], bs_ref[1, last]
-    sees_new = (bs_ref[3, last] > 0) & (bs_ref[2, q0] < new)
-    sees_all = (low_last <= 0) & (high_first >= cached)
-
-    @pl.when(sees_all)
-    def _():
-        old = scores_of(0, cached, 0, None, None)
-        late = scores_of(cached, new, 0, bv_ref[2:3, :], bv_ref[3:4, :])
-        kept = []
-        for h in range(heads):
-            top = jnp.maximum(top_of(old[h]), top_of(late[h]))
-            kept.append((jnp.exp2(old[h] * scale - top), jnp.exp2(late[h] * scale - top)))
-            m_s[h] = top
-        for h in range(heads):
-            w_old, w_late = kept[h]
-            l_s[h] = jnp.sum(w_old, axis=0, keepdims=True) + jnp.sum(w_late, axis=0, keepdims=True)
-            acc_s[h] = mixed(h, 0, w_old) + mixed(h, cached, w_late)
-
-    @pl.when(jnp.logical_not(sees_all))
-    def _():
-        m_s[...] = jnp.full_like(m_s, LOW).astype(BF16).astype(F32)
-        l_s[...] = jnp.zeros_like(l_s)
-        acc_s[...] = jnp.zeros_like(acc_s)
-
-        def add(first, count, base, low, high):
-            scores = scores_of(first, count, base, low, high)
+    def one_tile(t, carry):
+        q0 = pl.multiple_of(t * rows, rows)
+        last = q0 + rows - 1
+        lanes = pl.ds(q0, rows)
+        low_first, low_last = bs_ref[0, q0], bs_ref[0, last]
+        high_first, high_last = bs_ref[1, q0], bs_ref[1, last]
+        sees_new = (bs_ref[3, last] > 0) & (bs_ref[2, q0] < new)
+        sees_all = (low_last <= 0) & (high_first >= cached)
+        begin = lax.div(low_first, block)
+        end = jnp.where(high_last > low_first, lax.div(high_last + block - 1, block), begin)
+        sees_much = end - begin > 2
+
+        def scores_of(first, count, base, masks):
+            found = []
+            for h in range(heads):
+                scores = lax.dot_general(
+                    k_ref[pl.ds(first, count), columns(h)],
+                    q_ref[lanes, columns(h)],
+                    (((1,), (1,)), ((), ())),
+                    preferred_element_type=F32,
+                )
+                if masks is not None:
+                    at = lax.broadcasted_iota(jnp.int32, scores.shape, 0) + base
+                    low, high = (bv_ref[m : m + 1, lanes] for m in masks)
+                    scores = jnp.where((at >= low) & (at < high), scores, HIDE)
+                found.append(scores)
+            return found
+
+        def one_pass(masks):
+            old = scores_of(0, cached, 0, masks)
+            late = scores_of(cached, new, 0, (2, 3))
             kept = []
             for h in range(heads):
-                m_old = m_s[h]
-                m_new = jnp.maximum(m_old, top_of(scores[h]))
-                weights = jnp.exp2(scores[h] * scale - m_new)
-                fade = jnp.exp2(m_old - m_new)
-                m_s[h] = m_new
-                l_s[h] = l_s[h] * fade + jnp.sum(weights, axis=0, keepdims=True)
-                kept.append((fade, weights))
+                top = jnp.maximum(jnp.maximum(top_of(old[h]), top_of(late[h])), LOW)
+                top = top.astype(BF16).astype(F32)
+                kept.append((jnp.exp2(old[h] * scale - top), jnp.exp2(late[h] * scale - top)))
+                m_s[h] = top
             for h in range(heads):
-                fade, weights = kept[h]
-                acc_s[h] = acc_s[h] * fade + mixed(h, first, weights)
-
-        begin = lax.div(low_first, block)
-        end = jnp.where(high_last > low_first, lax.div(high_last + block - 1, block), begin)
-
-        def one_block(b, carry):
-            first = pl.multiple_of(b * block, block)
-            whole = (low_last <= first) & (high_first >= first + block)
-
-            @pl.when(whole)
+                w_old, w_late = kept[h]
+                l_s[h] = jnp.sum(w_old, axis=0, keepdims=True) + jnp.sum(w_late, axis=0, keepdims=True)
+                acc_s[h] = mixed(h, 0, w_old) + mixed(h, cached, w_late)
+
+        @pl.when(sees_all)
+        def _():
+            one_pass(None)
+
+        @pl.when(jnp.logical_not(sees_all) & sees_much)
+        def _():
+            one_pass((0, 1))
+
+        @pl.when(jnp.logical_not(sees_all) & jnp.logical_not(sees_much))
+        def _():
+            m_s[...] = jnp.full_like(m_s, LOW).astype(BF16).astype(F32)
+            l_s[...] = jnp.zeros_like(l_s)
+            acc_s[...] = jnp.zeros_like(acc_s)
+
+            def add(first, count, base, masks):
+                scores = scores_of(first, count, base, masks)
+                kept = []
+                for h in range(heads):
+                    m_old = m_s[h]
+                    m_new = jnp.maximum(m_old, top_of(scores[h]))
+                    weights = jnp.exp2(scores[h] * scale - m_new)
+                    fade = jnp.exp2(m_old - m_new)
+                    m_s[h] = m_new
+                    l_s[h] = l_s[h] * fade + jnp.sum(weights, axis=0, keepdims=True)
+                    kept.append((fade, weights))
+                for h in range(heads):
+                    fade, weights = kept[h]
+                    acc_s[h] = acc_s[h] * fade + mixed(h, first, weights)
+
+            def one_block(b, carry):
+                first = pl.multiple_of(b * block, block)
+                add(first, block, first, (0, 1))
+                return carry
+
+            lax.fori_loop(begin, end, one_block, 0)
+
+            @pl.when(sees_new)
             def _():
-                add(first, block, first, None, None)
-
-            @pl.when(jnp.logical_not(whole))
-            def _():
-                add(first, block, first, bv_ref[0:1, :], bv_ref[1:2, :])
-
-            return carry
-
-        lax.fori_loop(begin, end, one_block, 0)
-
-        @pl.when(sees_new)
-        def _():
-            add(cached, new, 0, bv_ref[2:3, :], bv_ref[3:4, :])
-
-    for h in range(heads):
-        pack(o_ref.at[0, h], acc_s[h], m_s[h], l_s[h])
+                add(cached, new, 0, (2, 3))
+
+        for h in range(heads):
+            for y in (0, 1):
+                cols = slice(y * rows // 2, (y + 1) * rows // 2)
+                pack(o_ref.at[t, h, y], acc_s[h, :, cols], m_s[h, :, cols], l_s[h, :, cols])
+        return carry
+
+    lax.fori_loop(0, o_ref.shape[0], one_tile, 0)
 
 
 def pack(ref, out, top, total):
@@ -371,15 +399,22 @@
     patch_out, byte_out,
     hidden, w_ref, dkv_in, dkv, gain_ref, kgain, qgain, dqw_ref, dow_ref, states_ref, nr,
     ring_in, ring_out, last, last_in, att, rs_out, rs_in, ag_in, kv_tile, kvg, bq_tile, bq,
-    bp_both, mix_tile, mix, bs_out, bs_in, send_sem, recv_sem, local_sem,
+    bp_both, span, mix_tile, mix, bs_out, bs_in, send_sem, recv_sem, local_sem,
 ):
     place = Place(zn)
     sends, loads = Sends(send_sem, recv_sem), Loads(local_sem)
     k, z, yl = place.k, place.z, place.yl
     me = lax.axis_index("head")
     peer = place.device(0, False, True)
-    others = [lax.rem(me + i, hn) for i in range(1, hn)]
-    sources = [me] + [lax.rem(me + hn - i, hn) for i in range(1, hn)]
+    x, yh = lax.div(me, 2), lax.rem(me, 2)
+    xn = hn // 2
+    ways = [(dx, dy) for dy in (1, 0) for dx in sorted(range(xn), key=lambda n: -min(n, xn - n)) if dx or dy]
+
+    def head_at(dx, dy):
+        return lax.rem(x + dx + xn, xn) * 2 + (1 - yh if dy else yh)
+
+    others = [head_at(dx, dy) for dx, dy in ways]
+    sources = [me] + [head_at(-dx, dy) for dx, dy in ways]
     for_queries = [
         loads.start(a, b)
         for a, b in ((states_hbm, states_ref), (dqw_hbm, dqw_ref), (qgain_hbm, qgain), (bp_hbm, bp_both.at[k]))
@@ -390,10 +425,10 @@
         loads.start(a, b)
         for a, b in ((gain_hbm, gain_ref), (kgain_hbm, kgain), (nr_hbm, nr), (dow_hbm, dow_ref))
     ]
-    greet(place.near() + [{"head": d} for d in others])
+    greet(place.near(line_steps(zn)) + [{"head": d} for d in others])
     new, slice_width = hidden.shape
     heads = part.shape[1]
-    dim = part.shape[2] - 16
+    dim = part.shape[3] - 16
     bytes_, half = states_ref.shape[0], kgain.shape[1]
 
     swapped = []
@@ -421,42 +456,43 @@
 
     idle = [byte_queries, flat_weights]
     far, near = zn // 2, zn - 1 - zn // 2
-    counts = [(far, near) if h % 2 == 0 else (near, far) for h in range(heads)]
+    chains = [(h, y) for h in range(heads) for y in (0, 1)]
+    counts = {(h, y): (far, near) if h % 2 == 0 else (near, far) for h, y in chains}
     made = {}
     for step in range(max(far, near)):
-        for h in range(heads):
+        for chain in chains:
             for way in (0, 1):
-                count = counts[h][way]
+                count = counts[chain][way]
                 if step >= count:
                     continue
                 sign = 1 - 2 * way
                 target = place.around(sign * (count - step))
                 if step == 0:
-                    src = part.at[target, h]
+                    src = part.at[target, *chain]
                 else:
-                    made[h, way, step - 1].receive()
-                    src = ring_out.at[h, way, step]
-                    pack(src, *merged([unpack(part.at[target, h]), unpack(ring_in.at[h, way, step - 1])]))
-                made[h, way, step] = sends.make(src, ring_in.at[h, way, step], place.device(sign, False, 0))
+                    made[chain, way, step - 1].receive()
+                    src = ring_out.at[*chain, way, step]
+                    pack(src, *merged([unpack(part.at[target, *chain]), unpack(ring_in.at[*chain, way, step - 1])]))
+                made[chain, way, step] = sends.make(
+                    src, ring_in.at[*chain, way, step], place.device(sign, False, 0)
+                )
         if step < len(idle):
             idle[step]()
     for work in idle[max(far, near) :]:
         work()
-    summed = []
-    for h in range(heads):
-        got = [unpack(part.at[z, h])]
+    summed = {}
+    for chain in chains:
+        got = [unpack(part.at[z, *chain])]
         for way in (0, 1):
-            count = counts[h][way]
+            count = counts[chain][way]
             if count:
-                made[h, way, count - 1].receive()
-                got.append(unpack(ring_in.at[h, way, count - 1]))
-        summed.append(merged(got))
+                made[chain, way, count - 1].receive()
+                got.append(unpack(ring_in.at[*chain, way, count - 1]))
+        summed[chain] = merged(got)
     for y in (0, 1):
-        cols = slice(y * 2 * new, (y + 1) * 2 * new)
         for core in (0, 1):
             joined = []
-            for a, b in zip(*summed):
-                a, b = a[:, cols], b[:, cols]
+            for a, b in zip(summed[0, y], summed[1, y]):
                 lane = lax.broadcasted_iota(jnp.int32, a.shape, 1)
                 if core == 0:
                     joined.append(jnp.where(lane < new, a, pltpu.roll(b, new, 1)))
@@ -515,41 +551,43 @@
     kv_tile[0] = jnp.where(lane < half, keys, pltpu.roll(values, half, 1)).astype(BF16)
     kv_tile[1] = jnp.where(lane < half, pltpu.roll(keys, half, 1), values).astype(BF16)
 
-    spans = []
-
     def byte_spans():
         swapped[0].receive()
-        owner = jnp.concatenate([bp_both[0], bp_both[1]], axis=1)
-        first = jnp.zeros(owner.shape, F32)
+        owners = bp_both[...]
+        first = jnp.zeros(owners.shape, F32)
         mates = nr[...]
         for r in range(1, 8):
-            begins = jnp.sum(jnp.where(mates < r, 1.0, 0.0), axis=1, keepdims=True)
-            first = jnp.where(owner.astype(F32) >= begins, begins, first)
-        spans.append((first.astype(jnp.int32), owner))
-
-    ring_gather(sends, place, kv_tile, kvg, [byte_spans])
+            begins = jnp.sum(jnp.where(mates < r, 1.0, 0.0), axis=1, keepdims=True)[None]
+            first = jnp.where(owners.astype(F32) >= begins, begins, first)
+        span[...] = first.astype(jnp.int32)
+
+    line_gather(sends, place, kv_tile, kvg, [byte_spans])
     for copy in sends.made:
         copy.receive()
-    first, owner = spans[0]
-
-    queries = bq[...]
+    spans = (span, bp_both)
+
     block = min(512, kvg.shape[0])
     scale = half ** (-0.5) * LOG2E
-    out, total = 0.0, 0.0
-    for b in range(kvg.shape[0] // block):
-        kv = kvg[b * block : (b + 1) * block, :]
-        scores = lax.dot_general(kv, queries, (((1,), (1,)), ((), ())), preferred_element_type=F32)
-        at = lax.broadcasted_iota(jnp.int32, scores.shape, 0) + b * block
-        weights = jnp.where((at >= first) & (at <= owner), jnp.exp2(scores * scale), 0.0)
-        total = total + jnp.sum(weights, axis=0, keepdims=True)
-        out = out + lax.dot_general(
-            kv, weights.astype(BF16), (((0,), (0,)), ((), ())), preferred_element_type=F32
-        )
-    mix_tile[...] = (out[half:, :] / total).astype(BF16)
+
+    def byte_attention(core):
+        queries = bq[aligned(core * bytes_, bytes_), :]
+        first, owner = spans[0][core], spans[1][core]
+        out, total = 0.0, 0.0
+        for b in range(kvg.shape[0] // block):
+            kv = kvg[b * block : (b + 1) * block, :]
+            scores = lax.dot_general(kv, queries, (((1,), (1,)), ((), ())), preferred_element_type=F32)
+            at = lax.broadcasted_iota(jnp.int32, scores.shape, 0) + b * block
+            weights = jnp.where((at >= first) & (at <= owner), jnp.exp2(scores * scale), 0.0)
+            total = total + jnp.sum(weights, axis=0, keepdims=True)
+            out = out + lax.dot_general(
+                kv, weights.astype(BF16), (((0,), (0,)), ((), ())), preferred_element_type=F32
+            )
+        return (out[half:, :] / total).astype(BF16)
+
     mix_rows = aligned(k * half, half)
-    theirs, ours = aligned((1 - k) * bytes_, bytes_), aligned(k * bytes_, bytes_)
-    mix_send = sends.make(mix_tile.at[:, theirs], mix.at[mix_rows, :], peer)
-    mix[mix_rows, :] = mix_tile[:, ours]
+    mix_tile[...] = byte_attention(1 - k)
+    mix_send = sends.make(mix_tile, mix.at[mix_rows, :], peer)
+    mix[mix_rows, :] = byte_attention(k)
     mix_send.receive()
     mixed = mix[...]
     out_width = byte_out.shape[1]
@@ -599,7 +637,7 @@
     slice_width = patch_hidden.shape[1]
     held = cache_request.reshape(8, cached // 8)
     mates = new_request.reshape(1, total)
-    gather_copies = 1 + 4 + 7 + 2 * zn
+    gather_copies = 1 + 4 + 7 + 4 * zn
     gathered, keys, values, bounds = pl.pallas_call(
         functools.partial(spread, zn),
         out_shape=(
@@ -631,17 +669,10 @@
     tile = 4 * new
     block = min(512, cached)
     partial = pl.pallas_call(
-        functools.partial(attend, 2 * cached, block, dim ** (-0.5) * LOG2E),
-        out_shape=jax.ShapeDtypeStruct((zn, heads // 2, dim + 16, tile), BF16),
-        grid=(zn,),
-        in_specs=[
-            pl.BlockSpec((tile, pair), lambda t: (t, 0)),
-            pl.BlockSpec((all_keys, pair), lambda t: (0, 0)),
-            pl.BlockSpec((all_keys, pair), lambda t: (0, 0)),
-            pl.BlockSpec((8, tile), lambda t: (0, t)),
-            pl.BlockSpec(memory_space=pltpu.SMEM),
-        ],
-        out_specs=pl.BlockSpec((1, heads // 2, dim + 16, tile), lambda t: (t, 0, 0, 0)),
+        functools.partial(attend, tile, 2 * cached, block, dim ** (-0.5) * LOG2E),
+        out_shape=jax.ShapeDtypeStruct((zn, heads // 2, 2, dim + 16, 2 * new), BF16),
+        in_specs=[in_vmem()] * 4 + [pl.BlockSpec(memory_space=pltpu.SMEM)],
+        out_specs=in_vmem(),
         scratch_shapes=[
             VMEM((heads // 2, 1, tile), F32),
             VMEM((heads // 2, 1, tile), F32),
@@ -658,7 +689,7 @@
     half = dec_width // 2
     steps = max(zn // 2, 1)
     peers = max(hn - 1, 1)
-    finish_copies = 2 + 2 * (zn - 1) + 3 + 3 * (hn - 1) + 7 + 2 * zn + 1
+    finish_copies = 2 + 4 * (zn - 1) + 3 + 3 * (hn - 1) + 3 + 3 * (zn - 1) + 1
     flat_weight = out_weight.reshape(heads * dim, -1)
     return pl.pallas_call(
         functools.partial(finish, zn, hn),
@@ -680,8 +711,8 @@
             VMEM(dec_out_weight.shape, BF16),
             VMEM(byte_states.shape, BF16),
             VMEM((1, total), jnp.int32),
-            VMEM((heads // 2, 2, steps, dim + 16, tile), BF16),
-            VMEM((heads // 2, 2, steps, dim + 16, tile), BF16),
+            VMEM((heads // 2, 2, 2, steps, dim + 16, 2 * new), BF16),
+            VMEM((heads // 2, 2, 2, steps, dim + 16, 2 * new), BF16),
             VMEM((2, 2, dim + 16, 2 * new), BF16),
             VMEM((3, dim + 16, 2 * new), BF16),
             VMEM((new, heads * dim), BF16),
@@ -693,7 +724,8 @@
             VMEM((2, bytes_, dec_width), BF16),
             VMEM((2 * bytes_, dec_width), BF16),
             VMEM((2, 1, bytes_), jnp.int32),
-            VMEM((half, 2 * bytes_), BF16),
+            VMEM((2, 1, bytes_), jnp.int32),
+            VMEM((half, bytes_), BF16),
             VMEM((dec_width, bytes_), BF16),
             VMEM((peers, bytes_, out_width), BF16),
             VMEM((peers, bytes_, out_width), BF16),

time: 125 us -> 117 us (0.936)
  Pallas kernels: 116 us -> 109 us
    pallas_call x1, Pallas kernels: 14.9 us -> 11.5 us  [per_device(): pl.pallas_call(functools.partial(attend, tile, 2 * cached, block, dim **...]
    pallas_call x1, Pallas kernels: 76 us -> 73.4 us  [per_device(): pl.pallas_call(functools.partial(finish, zn, hn), out_shape=(jax.ShapeDty...]
    pallas_call x1, Pallas kernels: 25.4 us -> 23.6 us  [per_device(): pl.pallas_call(functools.partial(spread, zn), out_shape=(jax.ShapeDtypeSt...]
where the time goes in v3:
time: 117 us
  Pallas kernels  109 us (93%)
  local copies, waits for them, and re-layouts  7.67 us (7%)
    pallas_call x1, Pallas kernels, per_device(): pl.pallas_call(functools.partial(finish, zn, hn), out_shape=(jax.ShapeDty...  73.4 us
    pallas_call x1, Pallas kernels, per_device(): pl.pallas_call(functools.partial(spread, zn), out_shape=(jax.ShapeDtypeSt...  23.6 us
    pallas_call x1, Pallas kernels, per_device(): pl.pallas_call(functools.partial(attend, tile, 2 * cached, block, dim **...  11.5 us
    unnamed x36, local copies, waits for them, and re-layouts  7.67 us

profile of v3, /device:TPU:1, one launch (start us, length us, event | category | flops | bytes accessed | tf_op | source)
XLA Modules:
  0.0 117.1 jit_solution(3338193906366083366)
XLA Ops:
  0.6 0.0 copy-start.1
  0.6 1.2 %copy-done.1 = bf16[1024,4,128]{2,1,0:T(4,128)(2,1)S(1)} copy-done((bf16[1024,4,128]{2,1,0:T(4,128)(2,1)S(1)}, bf16[1024,4,128]{2,1,0:T(4,128)(2,1)}, u32[]{:S(2)}) %copy-start.1) | copy-done | bytes 1048600
  1.9 1.2 %copy-done.2 = bf16[1024,4,128]{2,1,0:T(4,128)(2,1)S(1)} copy-done((bf16[1024,4,128]{2,1,0:T(4,128)(2,1)S(1)}, bf16[1024,4,128]{2,1,0:T(4,128)(2,1)}, u32[]{:S(2)}) %copy-start.2) | copy-done | bytes 1048600
  3.1 0.8 copy-done.7
  3.9 0.8 copy-done.8
  4.8 0.8 copy-done.9
  5.6 0.7 copy-done.10
  6.3 0.7 copy-done.13
  7.0 23.6 %spread.1 = (bf16[2048,256]{1,0:T(8,128)(2,1)S(1)}, bf16[2176,256]{1,0:T(8,128)(2,1)S(1)}, bf16[2176,256]{1,0:T(8,128)(2,1)S(1)}, s32[8,2048]{1,0:T(8,128)S(1)}) custom-call(bf16[64,4,128]{2,1,0:T(4,128)(2,1)S(1)} %copy-done.7, bf16[64,4,128]{2,1,0:T(4,128)(2,1)S(1)} %copy-done.8, bf16[64,4,128]{2,1,0:T(4,128)(2,1)S(1)} %copy-done.9, ...), custom_call_target="tpu_custom_call" | custom-call | tf_op jit(solution)/shard_map/spread/pallas_call | solution.py:641
  30.6 0.0 copy-start
  30.7 0.0 copy-start.3
  30.7 0.0 copy-start.4
  30.7 0.0 copy-start.5
  30.7 0.0 copy-start.6
  30.7 0.0 copy-start.11
  30.7 0.0 copy-start.12
  30.7 0.0 copy-start.14
  30.7 0.0 copy-start.15
  30.7 0.0 copy-start.16
  30.8 11.5 %attend.1.part = bf16[8,2,2,144,128]{4,3,2,1,0:T(8,128)(2,1)S(1)} custom-call(bf16[2048,256]{1,0:T(8,128)(2,1)S(1)} %get-tuple-element.6.q_ref, bf16[2176,256]{1,0:T(8,128)(2,1)S(1)} %get-tuple-element.7.k_ref, bf16[2176,256]{1,0:T(8,128)(2,1)S(1)} %get-tuple-element.8.v_ref, s32[8,2048]{1,0:T(8,128)S(1)} %get-tuple-element.9.bv_ref.bs_ref, ...), custom_call_target="tpu_custom_call" | custom-call | tf_op jit(solution)/shard_map/attend/pallas_call | solution.py:671
  42.3 0.0 copy-done
  42.4 73.4 %finish.1 = (bf16[64,512]{1,0:T(8,128)(2,1)S(1)}, bf16[256,128]{1,0:T(8,128)(2,1)S(1)}) custom-call(bf16[8,2,2,144,128]{4,3,2,1,0:T(8,128)(2,1)S(1)} %attend.1.part, bf16[64,512]{1,0:T(8,128)(2,1)S(1)} %copy-done.6, bf16[512,4096]{1,0:T(8,128)(2,1)} %bitcast.14, bf16[4096,2,128]{2,1,0:T(2,128)(2,1)S(1)} %copy-done, f32[1,4096]{1,0:T(1,128)S(1)} %bitcast.9, ...), custom_call_target="tpu_custom_call" | custom-call | tf_op jit(solution)/shard_map/finish/pallas_call | solution.py:694
  115.8 0.6 copy.21
  116.5 0.6 copy.22
  (15 shorter events, 0.0 us)
Async XLA Ops:
  0.6 1.2 %copy-start.1 = (bf16[1024,4,128]{2,1,0:T(4,128)(2,1)S(1)}, bf16[1024,4,128]{2,1,0:T(4,128)(2,1)}, u32[]{:S(2)}) copy-start(bf16[1024,4,128]{2,1,0:T(4,128)(2,1)} %ck_hbm.1) | copy-start | bytes 3145732
  1.9 1.2 %copy-start.2 = (bf16[1024,4,128]{2,1,0:T(4,128)(2,1)S(1)}, bf16[1024,4,128]{2,1,0:T(4,128)(2,1)}, u32[]{:S(2)}) copy-start(bf16[1024,4,128]{2,1,0:T(4,128)(2,1)} %cv_hbm.1) | copy-start | bytes 3145732
  3.1 0.8 copy-start.7
  3.9 0.8 copy-start.8
  4.8 0.8 copy-start.9
  5.6 0.7 copy-start.10
  6.3 0.7 copy-start.13
  30.6 11.7 %copy-start = (bf16[4096,2,128]{2,1,0:T(2,128)(2,1)S(1)}, bf16[4096,2,128]{2,1,0:T(2,128)(2,1)}, u32[]{:S(2)}) copy-start(bf16[4096,2,128]{2,1,0:T(2,128)(2,1)} %dkv_hbm.1) | copy-start | bytes 6291460
  30.7 11.7 %copy-start.3 = (bf16[256,1024]{1,0:T(8,128)(2,1)S(1)}, bf16[256,1024]{1,0:T(8,128)(2,1)}, u32[]{:S(2)}) copy-start(bf16[256,1024]{1,0:T(8,128)(2,1)} %states_hbm.1) | copy-start | bytes 1572868
  30.7 11.7 %copy-start.4 = (bf16[1024,128]{1,0:T(8,128)(2,1)S(1)}, bf16[1024,128]{1,0:T(8,128)(2,1)}, u32[]{:S(2)}) copy-start(bf16[1024,128]{1,0:T(8,128)(2,1)} %dqw_hbm.1) | copy-start | bytes 786436
  30.7 11.7 %copy-start.5 = (bf16[128,1024]{1,0:T(8,128)(2,1)S(1)}, bf16[128,1024]{1,0:T(8,128)(2,1)}, u32[]{:S(2)}) copy-start(bf16[128,1024]{1,0:T(8,128)(2,1)} %dow_hbm.1) | copy-start | bytes 786436
  30.7 11.7 %copy-start.6 = (bf16[64,512]{1,0:T(8,128)(2,1)S(1)}, bf16[64,512]{1,0:T(8,128)(2,1)}, u32[]{:S(2)}) copy-start(bf16[64,512]{1,0:T(8,128)(2,1)} %hidden_hbm.1) | copy-start | bytes 196612
  30.7 11.7 %copy-start.11 = (s32[2048]{0:T(1024)S(1)}, s32[2048]{0:T(1024)}, u32[]{:S(2)}) copy-start(s32[2048]{0:T(1024)} %param.24) | copy-start | bytes 24580
  30.7 11.7 %copy-start.12 = (f32[4096]{0:T(1024)S(1)}, f32[4096]{0:T(1024)}, u32[]{:S(2)}) copy-start(f32[4096]{0:T(1024)} %param.26) | copy-start | bytes 49156
  30.7 11.7 %copy-start.14 = (s32[256]{0:T(256)S(1)}, s32[256]{0:T(256)}, u32[]{:S(2)}) copy-start(s32[256]{0:T(256)} %param.33) | copy-start | bytes 3076
  30.7 11.7 %copy-start.15 = (f32[64]{0:T(128)S(1)}, f32[64]{0:T(128)}, u32[]{:S(2)}) copy-start(f32[64]{0:T(128)} %param.30) | copy-start | bytes 772
  30.7 11.7 %copy-start.16 = (f32[64]{0:T(128)S(1)}, f32[64]{0:T(128)}, u32[]{:S(2)}) copy-start(f32[64]{0:T(128)} %param.29) | copy-start | bytes 772

commit v4 on v3

v4 whole, which is shorter than its diff:
```python
import functools

import jax
import jax.numpy as jnp
from jax import lax
from jax.experimental import pallas as pl
from jax.experimental.pallas import tpu as pltpu
from jax.sharding import PartitionSpec as P

MESH = pl.DeviceIdType.MESH
VMEM = pltpu.VMEM
F32 = jnp.float32
BF16 = jnp.bfloat16
HIDE = -1e30
LIFT = 16384.0
LOG2E = 1.4426950408889634


def in_vmem():
    return pl.BlockSpec(memory_space=pltpu.VMEM)


def in_place():
    return pl.BlockSpec(memory_space=pltpu.HBM)


class Place:
    def __init__(self, zn):
        c = lax.axis_index("ctx")
        self.c = c
        self.zn = zn
        self.z = lax.div(c, 4)
        self.yl = lax.rem(lax.div(c, 2), 2)
        self.k = lax.rem(c, 2)
        self.cores = (self.k, 1 - self.k)

    def around(self, step):
        return lax.rem(self.z + (step + 2 * self.zn), self.zn)

    def device(self, step, other_y, other_core):
        y = 1 - self.yl if other_y else self.yl
        return {"ctx": self.around(step) * 4 + y * 2 + self.cores[other_core]}

    def near(self, steps):
        found = [self.device(0, False, True)]
        for core in (False, True):
            found.append(self.device(0, True, core))
            found += [self.device(step, False, core) for step in steps]
        return found


class Copy:
    def __init__(self, dma):
        self.dma, self.got = dma, False

    def start(self):
        self.dma.start()
        return self

    def receive(self):
        if not self.got:
            self.dma.wait_recv()
        self.got = True


class Sends:
    def __init__(self, send_sem, recv_sem):
        self.send_sem, self.recv_sem, self.made = send_sem, recv_sem, []

    def make(self, src, dst, device):
        at = len(self.made)
        copy = Copy(
            pltpu.make_async_remote_copy(
                src_ref=src,
                dst_ref=dst,
                send_sem=self.send_sem.at[at],
                recv_sem=self.recv_sem.at[at],
                device_id=device,
                device_id_type=MESH,
            )
        )
        self.made.append(copy)
        return copy.start()

    def close(self):
        for copy in self.made:
            copy.receive()
        for copy in self.made:
            copy.dma.wait_send()


class Loads:
    def __init__(self, sem):
        self.sem, self.used = sem, 0

    def start(self, src, dst):
        copy = pltpu.make_async_copy(src, dst, self.sem.at[self.used])
        self.used += 1
        copy.start()
        return copy


def greet(devices):
    barrier = pltpu.get_barrier_semaphore()
    for device in devices:
        pl.semaphore_signal(barrier, inc=1, device_id=device, device_id_type=MESH)
    pl.semaphore_wait(barrier, len(devices))


def aligned(start, size):
    return pl.ds(pl.multiple_of(start, size), size)


def first_hop(sends, place, source, buffer, step, other_y, cores):
    rows = source.shape[1]
    mine = buffer.at[aligned(place.c * rows, rows), :]
    return [sends.make(source.at[place.cores[core]], mine, place.device(step, other_y, core)) for core in cores]


def ring_gather(sends, place, source, buffer, early, work):
    zn = place.zn
    rows = source.shape[1]
    far, near = zn // 2, zn - 1 - zn // 2
    arrived = {}
    for way, count in ((1, far), (-1, near)):
        if count:
            for core, copy in enumerate(first_hop(sends, place, source, buffer, way, False, (0, 1))):
                arrived[0, core, way, 0] = copy
    from_y = first_hop(sends, place, source, buffer, 0, True, (0, 1))
    from_core = first_hop(sends, place, source, buffer, 0, False, (1,))
    buffer[aligned(place.c * rows, rows), :] = source[place.k]
    early()
    for turn in range(far + 1):
        for stream, step in ((0, turn + 1), (1, turn)):
            y = place.yl if stream == 0 else 1 - place.yl
            counts = (far, near) if stream == 0 else (near, far)
            for core in (0, 1):
                for way, count in zip((1, -1), counts):
                    if step >= count:
                        continue
                    (arrived[stream, core, way, step - 1] if step else from_y[core]).receive()
                    owner = place.around(-way * step) * 4 + y * 2 + place.cores[core]
                    piece = buffer.at[aligned(owner * rows, rows), :]
                    arrived[stream, core, way, step] = sends.make(piece, piece, place.device(way, False, 0))
        if turn == 0:
            for copy in from_y + from_core:
                copy.receive()
        for (_, _, _, step), copy in list(arrived.items()):
            if step == turn - 1:
                copy.receive()
        work(turn)


def line_steps(zn):
    return sorted([way * n for n in range(1, zn // 2 + 1) for way in (1, -1) if 2 * n < zn or way > 0], key=lambda n: -abs(n))


def line_gather(sends, place, source, buffer, idle=()):
    rows = source.shape[1]
    found = {}
    for step in line_steps(place.zn):
        found[step] = first_hop(sends, place, source, buffer, step, False, (0, 1))
    found[0] = first_hop(sends, place, source, buffer, 0, False, (1,))
    first_hop(sends, place, source, buffer, 0, True, (0, 1))
    buffer[aligned(place.c * rows, rows), :] = source[place.k]
    for work in idle:
        work()
    for step in reversed(line_steps(place.zn)):
        for copy in found[step]:
            copy.receive()
        chip = place.around(-step) * 2 + place.yl
        piece = buffer.at[aligned(chip * 2 * rows, 2 * rows), :]
        sends.make(piece, piece, place.device(0, True, False))


def pack(ref, out, top, total):
    dim = out.shape[0]
    ref[0:dim, :] = out.astype(BF16)
    coarse = total.astype(BF16).astype(F32)
    row = lax.broadcasted_iota(jnp.int32, (16, out.shape[1]), 0)
    tail = jnp.where(row == 0, top, jnp.where(row == 1, coarse, jnp.where(row == 2, total - coarse, 0.0)))
    ref[dim : dim + 16, :] = tail.astype(BF16)


def unpack(ref):
    value = ref[...]
    dim = value.shape[0] - 16
    tail = value[dim:, :].astype(F32)
    return value[:dim, :].astype(F32), tail[0:1, :], tail[1:2, :] + tail[2:3, :]


def merged(parts):
    top = parts[0][1]
    for part in parts[1:]:
        top = jnp.maximum(top, part[1])
    out, total = 0.0, 0.0
    for o, m, l in parts:
        factor = jnp.exp2(m - top)
        out = out + o * factor
        total = total + l * factor
    return out, top, total


def head_norm(values, gain, half):
    lane = lax.broadcasted_iota(jnp.int32, values.shape, 1)
    first = lane < half
    squares = values * values
    s0 = jnp.sum(jnp.where(first, squares, 0.0), axis=1, keepdims=True)
    s1 = jnp.sum(jnp.where(first, 0.0, squares), axis=1, keepdims=True)
    return values * lax.rsqrt(jnp.where(first, s0, s1) / half + 1e-6) * gain


def solve(
    zn, hn, q_hbm, nk_hbm, nv_hbm, ck_hbm, cv_hbm, cr_hbm,
    hidden_hbm, w_hbm, dkv_hbm, gain_hbm, kgain_hbm, qgain_hbm, dqw_hbm, dow_hbm, states_hbm, bp_hbm, nr_hbm,
    patch_out, byte_out,
    q_in, new_in, old_in, held, q_half, kv_half, qg, kc, vc, key_mark, query_mark, part,
    hidden, w_ref, dkv_in, dkv, gain_ref, kgain, qgain, dqw_ref, dow_ref, states_ref, nr,
    ring_in, ring_out, last, last_in, att, rs_out, rs_in, ag_in, kv_tile, kvg, bq_tile, bq,
    bp_both, span, mix_tile, mix, bs_out, bs_in, send_sem, recv_sem, local_sem,
):
    place = Place(zn)
    sends, loads = Sends(send_sem, recv_sem), Loads(local_sem)
    k, z, yl = place.k, place.z, place.yl
    me = lax.axis_index("head")
    peer = place.device(0, False, True)
    x, yh = lax.div(me, 2), lax.rem(me, 2)
    xn = hn // 2
    ways = [(dx, dy) for dy in (1, 0) for dx in sorted(range(xn), key=lambda n: -min(n, xn - n)) if dx or dy]

    def head_at(dx, dy):
        return lax.rem(x + dx + xn, xn) * 2 + (1 - yh if dy else yh)

    others = [head_at(dx, dy) for dx, dy in ways]
    sources = [me] + [head_at(-dx, dy) for dx, dy in ways]
    q_load = loads.start(q_hbm, q_in)
    kv_loads = [
        (loads.start(ck_hbm, old_in.at[0]), loads.start(nk_hbm, new_in.at[0])),
        (loads.start(cv_hbm, old_in.at[1]), loads.start(nv_hbm, new_in.at[1])),
    ]
    small = [loads.start(cr_hbm, held.at[k]), loads.start(nr_hbm, nr)]
    for_queries = [
        loads.start(a, b)
        for a, b in ((states_hbm, states_ref), (dqw_hbm, dqw_ref), (qgain_hbm, qgain), (bp_hbm, bp_both.at[k]))
    ]
    dkv_load = loads.start(dkv_hbm, dkv_in)
    w_loads = [loads.start(w_hbm, w_ref), loads.start(hidden_hbm, hidden)]
    late = [
        loads.start(a, b)
        for a, b in ((gain_hbm, gain_ref), (kgain_hbm, kgain), (dow_hbm, dow_ref))
    ]
    greet(place.near(line_steps(zn)) + [{"head": d} for d in others])
    new, slice_width = hidden.shape
    heads = part.shape[1]
    dim = part.shape[3] - 16
    bytes_, half = states_ref.shape[0], kgain.shape[1]
    cached = ck_hbm.shape[0]
    width = q_half.shape[2]
    chip = z * 2 + yl
    tile = 4 * new
    chip_first = chip * 2 * new
    scale = dim ** (-0.5) * LOG2E

    q_load.wait()
    flat = q_in[...].reshape(new, 2 * width)
    q_half[0] = flat[:, :width]
    q_half[1] = flat[:, width:]
    kept, swaps = [], []

    def swap(which, out):
        for copy in kv_loads[which]:
            copy.wait()
        for value, count, at, to in (
            (old_in[which], cached, 0, k * cached),
            (new_in[which], new, cached, 2 * cached + k * new),
        ):
            flat = value.reshape(count, 2 * width)
            rows = pl.ds(at, count)
            kv_half[which, 0, rows, :] = flat[:, :width]
            kv_half[which, 1, rows, :] = flat[:, width:]
            target = out.at[aligned(to, count), :]
            swaps.append(sends.make(kv_half.at[which, 1 - k, rows, :], target, peer))
            kept.append(loads.start(kv_half.at[which, k, rows, :], target))

    def marks(at, cuts):
        lane = lax.broadcasted_iota(jnp.int32, (1, query_mark.shape[1]), 1)
        low, high = jnp.zeros(lane.shape, F32), jnp.zeros(lane.shape, F32)
        for r in range(8):
            low = jnp.where(lane == r, cuts[r], low)
            high = jnp.where(lane == r, cuts[r + 1], high)
        return jnp.where((at >= low) & (at < high), 1.0, 0.0)

    def positions(count, first):
        return (lax.broadcasted_iota(jnp.int32, (count, query_mark.shape[1]), 0) + first).astype(F32)

    def early():
        for copy in small:
            copy.wait()
        held_swap = sends.make(held.at[k], held.at[k], peer)
        swap(0, kc)
        swap(1, vc)
        cuts = [
            jnp.sum(jnp.where(nr[...] < r, 1.0, 0.0), axis=1, keepdims=True) for r in range(9)
        ]
        query_mark[...] = marks(positions(query_mark.shape[0], 0), cuts).astype(BF16)
        key_mark[2 * cached :, :] = (LIFT * marks(positions(2 * new, chip_first), cuts)).astype(BF16)
        held_swap.receive()
        both = held[...]
        cuts = [
            jnp.sum(jnp.sum(jnp.where(both < r, 1.0, 0.0), axis=0), axis=(0, 1), keepdims=True)
            for r in range(9)
        ]
        key_mark[: 2 * cached, :] = (LIFT * marks(positions(2 * cached, 0), cuts)).astype(BF16)

    def attend(t):
        q0 = pl.multiple_of(t * tile, tile)
        rows = pl.ds(q0, tile)
        columns = [slice(h * dim, (h + 1) * dim) for h in range(heads)]
        scores = []
        for cols in columns:
            found = lax.dot_general(
                jnp.concatenate([kc[:, cols], key_mark[...]], axis=1),
                jnp.concatenate([qg[rows, cols], query_mark[rows, :]], axis=1),
                (((1,), (1,)), ((), ())),
                preferred_element_type=F32,
            )
            late = found[2 * cached :]
            at = lax.broadcasted_iota(jnp.int32, late.shape, 0) + chip_first
            asked = lax.broadcasted_iota(jnp.int32, late.shape, 1) + q0
            late = jnp.where(at <= asked, late, HIDE)
            scores.append(jnp.concatenate([found[: 2 * cached], late], axis=0))
        weights = []
        for found in scores:
            top = jnp.max(found, axis=0, keepdims=True) * scale - LIFT * scale
            top = top.astype(BF16).astype(F32)
            weights.append((top, jnp.exp2(found * scale - (top + LIFT * scale))))
        for h, (top, found) in enumerate(weights):
            total = jnp.sum(found, axis=0, keepdims=True)
            out = lax.dot_general(
                vc[:, columns[h]], found.astype(BF16), (((0,), (0,)), ((), ())), preferred_element_type=F32
            )
            for y in (0, 1):
                cols = slice(y * 2 * new, (y + 1) * 2 * new)
                pack(part.at[t, h, y], out[:, cols], top[:, cols], total[:, cols])

    far, near = zn // 2, zn - 1 - zn // 2
    chains = [(h, y) for h in range(heads) for y in (0, 1)]
    counts = {(h, y): (far, near) if h % 2 == 0 else (near, far) for h, y in chains}
    made = {}

    def reduce_step(step, chosen):
        for chain in chains:
            for way in (0, 1):
                count = counts[chain][way]
                if step >= count or count not in chosen:
                    continue
                sign = 1 - 2 * way
                target = place.around(sign * (count - step))
                if step == 0:
                    src = part.at[target, *chain]
                else:
                    made[chain, way, step - 1].receive()
                    src = ring_out.at[*chain, way, step]
                    pack(src, *merged([unpack(part.at[target, *chain]), unpack(ring_in.at[*chain, way, step - 1])]))
                made[chain, way, step] = sends.make(
                    src, ring_in.at[*chain, way, step], place.device(sign, False, 0)
                )

    def work(turn):
        if turn == 0:
            for copy in kept:
                copy.wait()
            for copy in swaps:
                copy.receive()
        if turn == far:
            reduce_step(0, (near,))

        def one(i, carry):
            attend(lax.rem(z + (1 - 2 * i) * turn + 2 * zn, zn))
            return carry

        lax.fori_loop(0, 1 if turn in (0, far) else 2, one, 0)
        if turn == far:
            reduce_step(0, (far,))

    ring_gather(sends, place, q_half, qg, early, work)

    swapped = []

    def byte_queries():
        for copy in for_queries:
            copy.wait()
        proj = jnp.dot(states_ref[...], dqw_ref[...], preferred_element_type=F32)
        gain = jnp.concatenate([qgain[...], qgain[...]], axis=1)
        normed = head_norm(proj, gain, half)
        lane = lax.broadcasted_iota(jnp.int32, normed.shape, 1)
        bq_tile[0] = jnp.where(lane < half, normed, 0.0).astype(BF16)
        bq_tile[1] = jnp.where(lane < half, pltpu.roll(normed, half, 1), 0.0).astype(BF16)
        rows = aligned(k * bytes_, bytes_)
        swapped.append(sends.make(bp_both.at[k], bp_both.at[k], peer))
        sends.make(bq_tile.at[1 - k], bq.at[rows, :], peer)
        bq[rows, :] = bq_tile[k]

    def flat_weights():
        dkv_load.wait()
        count = dkv.shape[0] // 4
        for i in range(4):
            rows = slice(i * count, (i + 1) * count)
            dkv[rows, :] = dkv_in[rows].reshape(count, dkv.shape[1])

    idle = [byte_queries, flat_weights]
    for step in range(max(far, 1)):
        if step:
            reduce_step(step, (far, near))
        if step < len(idle):
            idle[step]()
    for work_left in idle[max(far, 1) :]:
        work_left()
    summed = {}
    for chain in chains:
        got = [unpack(part.at[z, *chain])]
        for way in (0, 1):
            count = counts[chain][way]
            if count:
                made[chain, way, count - 1].receive()
                got.append(unpack(ring_in.at[*chain, way, count - 1]))
        summed[chain] = merged(got)
    for y in (0, 1):
        for core in (0, 1):
            joined = []
            for a, b in zip(summed[0, y], summed[1, y]):
                lane = lax.broadcasted_iota(jnp.int32, a.shape, 1)
                if core == 0:
                    joined.append(jnp.where(lane < new, a, pltpu.roll(b, new, 1)))
                else:
                    joined.append(jnp.where(lane < new, pltpu.roll(a, new, 1), b))
            pack(last.at[y, core], *joined)
    across = sends.make(last.at[1 - yl, k], last_in.at[0], place.device(0, True, False))
    beside = sends.make(last.at[yl, 1 - k], last_in.at[1], peer)
    diagonal = sends.make(last.at[1 - yl, 1 - k], last_in.at[2], place.device(0, True, True))
    for pair, parts, waits in (
        (k, (last.at[yl, k], last_in.at[0]), (across,)),
        (1 - k, (last_in.at[1], last_in.at[2]), (beside, diagonal)),
    ):
        for copy in waits:
            copy.receive()
        out, _, total = merged([unpack(ref) for ref in parts])
        turned = (out / total).T.astype(BF16)
        both = jnp.concatenate([turned[:new], turned[new:]], axis=1)
        att[:, aligned(pair * 2 * dim, 2 * dim)] = both

    for copy in w_loads:
        copy.wait()
    mine = att[...]

    def columns_for(d):
        return jnp.dot(mine, w_ref[:, aligned(d * slice_width, slice_width)], preferred_element_type=F32)

    rs_sends = []
    for i, d in enumerate(others):
        rs_out[i] = columns_for(d).astype(BF16)
        rs_sends.append(sends.make(rs_out.at[i], rs_in.at[i], {"head": d}))
    own = columns_for(me) + hidden[...].astype(F32)
    for i, copy in enumerate(rs_sends):
        copy.receive()
        own = own + rs_in[i].astype(F32)
    rounded = own.astype(BF16)
    ag_in[0] = rounded
    ag_sends = [sends.make(ag_in.at[0], ag_in.at[1 + i], {"head": d}) for i, d in enumerate(others)]
    patch_out[...] = rounded
    for copy in late:
        copy.wait()
    squares, proj = 0.0, 0.0
    for i, source in enumerate(sources):
        if i:
            ag_sends[i - 1].receive()
        wide = ag_in[i].astype(F32)
        squares = squares + jnp.sum(wide * wide, axis=1, keepdims=True)
        scaled = (wide * gain_ref[:, aligned(source * slice_width, slice_width)]).astype(BF16)
        rows = aligned(source * slice_width, slice_width)
        proj = proj + jnp.dot(scaled, dkv[rows, :], preferred_element_type=F32)
    proj = proj * lax.rsqrt(squares / (hn * slice_width) + 1e-5)
    keys = head_norm(proj[:, : 2 * half], jnp.concatenate([kgain[...], kgain[...]], axis=1), half)
    values = proj[:, 2 * half :]
    lane = lax.broadcasted_iota(jnp.int32, keys.shape, 1)
    kv_tile[0] = jnp.where(lane < half, keys, pltpu.roll(values, half, 1)).astype(BF16)
    kv_tile[1] = jnp.where(lane < half, pltpu.roll(keys, half, 1), values).astype(BF16)

    def byte_spans():
        swapped[0].receive()
        owners = bp_both[...]
        first = jnp.zeros(owners.shape, F32)
        mates = nr[...]
        for r in range(1, 8):
            begins = jnp.sum(jnp.where(mates < r, 1.0, 0.0), axis=1, keepdims=True)[None]
            first = jnp.where(owners.astype(F32) >= begins, begins, first)
        span[...] = first.astype(jnp.int32)

    line_gather(sends, place, kv_tile, kvg, [byte_spans])
    for copy in sends.made:
        copy.receive()
    spans = (span, bp_both)

    block = min(512, kvg.shape[0])
    byte_scale = half ** (-0.5) * LOG2E

    def byte_attention(core):
        queries = bq[aligned(core * bytes_, bytes_), :]
        first, owner = spans[0][core], spans[1][core]
        out, total = 0.0, 0.0
        for b in range(kvg.shape[0] // block):
            kv = kvg[b * block : (b + 1) * block, :]
            scores = lax.dot_general(kv, queries, (((1,), (1,)), ((), ())), preferred_element_type=F32)
            at = lax.broadcasted_iota(jnp.int32, scores.shape, 0) + b * block
            weights = jnp.where((at >= first) & (at <= owner), jnp.exp2(scores * byte_scale), 0.0)
            total = total + jnp.sum(weights, axis=0, keepdims=True)
            out = out + lax.dot_general(
                kv, weights.astype(BF16), (((0,), (0,)), ((), ())), preferred_element_type=F32
            )
        return (out[half:, :] / total).astype(BF16)

    mix_rows = aligned(k * half, half)
    mix_tile[...] = byte_attention(1 - k)
    mix_send = sends.make(mix_tile, mix.at[mix_rows, :], peer)
    mix[mix_rows, :] = byte_attention(k)
    mix_send.receive()
    mixed = mix[...]
    out_width = byte_out.shape[1]

    def byte_columns_for(d):
        cols = aligned(d * out_width, out_width)
        return lax.dot_general(mixed, dow_ref[:, cols], (((0,), (0,)), ((), ())), preferred_element_type=F32)

    bs_sends = []
    for i, d in enumerate(others):
        bs_out[i] = byte_columns_for(d).astype(BF16)
        bs_sends.append(sends.make(bs_out.at[i], bs_in.at[i], {"head": d}))
    own = byte_columns_for(me) + states_ref[:, aligned(me * out_width, out_width)].astype(F32)
    for i, copy in enumerate(bs_sends):
        copy.receive()
        own = own + bs_in[i].astype(F32)
    byte_out[...] = own.astype(BF16)
    sends.close()


def per_device(
    zn,
    hn,
    patch_hidden,
    queries,
    new_keys,
    new_values,
    cache_keys,
    cache_values,
    cache_request,
    new_request,
    out_weight,
    norm_gain,
    dec_kv_weight,
    dec_query_weight,
    query_gain,
    key_gain,
    dec_out_weight,
    byte_states,
    byte_patch,
):
    new, heads, dim = queries.shape
    cached = cache_keys.shape[0]
    total = new_request.shape[0]
    pair = heads // 2 * dim
    all_keys = 2 * (cached + new)
    slice_width = patch_hidden.shape[1]
    held = cache_request.reshape(8, cached // 8)
    mates = new_request.reshape(1, total)
    tile = 4 * new
    kv_rows = dec_kv_weight.shape[0]
    dec_width = dec_kv_weight.shape[2]
    bytes_ = byte_states.shape[0]
    out_width = dec_out_weight.shape[1] // hn
    half = dec_width // 2
    steps = max(zn // 2, 1)
    peers = max(hn - 1, 1)
    copies = 5 + 7 + 4 * zn + 2 + 4 * (zn - 1) + 3 + 3 * (hn - 1) + 3 + 3 * (zn - 1) + 1
    flat_weight = out_weight.reshape(heads * dim, -1)
    return pl.pallas_call(
        functools.partial(solve, zn, hn),
        out_shape=(
            jax.ShapeDtypeStruct(patch_hidden.shape, BF16),
            jax.ShapeDtypeStruct((bytes_, out_width), BF16),
        ),
        in_specs=[in_place()] * 17,
        out_specs=(in_vmem(), in_vmem()),
        scratch_shapes=[
            VMEM(queries.shape, BF16),
            VMEM((2, *new_keys.shape), BF16),
            VMEM((2, *cache_keys.shape), BF16),
            VMEM((2, *held.shape), jnp.int32),
            VMEM((2, new, pair), BF16),
            VMEM((2, 2, cached + new, pair), BF16),
            VMEM((total, pair), BF16),
            VMEM((all_keys, pair), BF16),
            VMEM((all_keys, pair), BF16),
            VMEM((all_keys, 128), BF16),
            VMEM((total, 128), BF16),
            VMEM((zn, heads // 2, 2, dim + 16, 2 * new), BF16),
            VMEM(patch_hidden.shape, BF16),
            VMEM(flat_weight.shape, BF16),
            VMEM(dec_kv_weight.shape, BF16),
            VMEM((kv_rows, 2 * dec_width), BF16),
            VMEM((1, kv_rows), F32),
            VMEM((1, half), F32),
            VMEM((1, half), F32),
            VMEM(dec_query_weight.shape, BF16),
            VMEM(dec_out_weight.shape, BF16),
            VMEM(byte_states.shape, BF16),
            VMEM((1, total), jnp.int32),
            VMEM((heads // 2, 2, 2, steps, dim + 16, 2 * new), BF16),
            VMEM((heads // 2, 2, 2, steps, dim + 16, 2 * new), BF16),
            VMEM((2, 2, dim + 16, 2 * new), BF16),
            VMEM((3, dim + 16, 2 * new), BF16),
            VMEM((new, heads * dim), BF16),
            VMEM((peers, new, slice_width), BF16),
            VMEM((peers, new, slice_width), BF16),
            VMEM((hn, new, slice_width), BF16),
            VMEM((2, new, dec_width), BF16),
            VMEM((total, dec_width), BF16),
            VMEM((2, bytes_, dec_width), BF16),
            VMEM((2 * bytes_, dec_width), BF16),
            VMEM((2, 1, bytes_), jnp.int32),
            VMEM((2, 1, bytes_), jnp.int32),
            VMEM((half, bytes_), BF16),
            VMEM((dec_width, bytes_), BF16),
            VMEM((peers, bytes_, out_width), BF16),
            VMEM((peers, bytes_, out_width), BF16),
            pltpu.SemaphoreType.DMA((copies,)),
            pltpu.SemaphoreType.DMA((copies,)),
            pltpu.SemaphoreType.DMA((24,)),
        ],
        compiler_params=pltpu.CompilerParams(
            collective_id=0, has_side_effects=True, vmem_limit_bytes=60 * 2**20
        ),
        name="solve",
    )(
        queries,
        new_keys,
        new_values,
        cache_keys,
        cache_values,
        held,
        patch_hidden,
        flat_weight,
        dec_kv_weight,
        norm_gain.reshape(1, kv_rows),
        key_gain.reshape(1, half),
        query_gain.reshape(1, half),
        dec_query_weight,
        dec_out_weight,
        byte_states,
        byte_patch.reshape(1, bytes_),
        mates,
    )


def solution(mesh):
    placed = (
        P("ctx", "head"),
        P("ctx", "head", None),
        P("ctx", "head", None),
        P("ctx", "head", None),
        P("ctx", "head", None),
        P("ctx", "head", None),
        P("ctx"),
        P(),
        P("head", None, None),
        P(),
        P(None, None, "head"),
        P(None, "head"),
        P(),
        P(),
        P("head", None),
        P("ctx", None),
        P("ctx"),
    )
    return jax.shard_map(
        functools.partial(per_device, mesh.shape["ctx"] // 4, mesh.shape["head"]),
        mesh=mesh,
        in_specs=placed,
        out_specs=(P("ctx", "head"), P("ctx", "head")),
        check_vma=False,
    )
```

time: 117 us -> 104 us (0.89)
  Pallas kernels: 109 us -> 100 us
  local copies, waits for them, and re-layouts: 7.67 us -> 2.95 us
    pallas_call x3 -> x1, Pallas kernels: 109 us -> 100 us  [per_device(): pl.pallas_call(functools.partial(solve, zn, hn), out_shape=(jax.ShapeDtyp...]
    unnamed x36 -> x2, local copies, waits for them, and re-layouts: 7.67 us -> 2.95 us
where the time goes in v4:
time: 104 us
  Pallas kernels  100 us (96%)
  local copies, waits for them, and re-layouts  2.95 us (3%)
    pallas_call x1, Pallas kernels, per_device(): pl.pallas_call(functools.partial(solve, zn, hn), out_shape=(jax.ShapeDtyp...  100 us
    unnamed x2, local copies, waits for them, and re-layouts  2.95 us

profile of v4, /device:TPU:1, one launch (start us, length us, event | category | flops | bytes accessed | tf_op | source)
XLA Modules:
  0.0 103.9 jit_solution(8325696127523207563)
XLA Ops:
  0.6 100.3 %solve.1 = (bf16[64,512]{1,0:T(8,128)(2,1)}, bf16[256,128]{1,0:T(8,128)(2,1)}) custom-call(bf16[64,4,128]{2,1,0:T(4,128)(2,1)} %q_hbm.1, bf16[64,4,128]{2,1,0:T(4,128)(2,1)} %nk_hbm.1, bf16[64,4,128]{2,1,0:T(4,128)(2,1)} %nv_hbm.1, bf16[1024,4,128]{2,1,0:T(4,128)(2,1)} %ck_hbm.1, bf16[1024,4,128]{2,1,0:T(4,128)(2,1)} %cv_hbm.1, s32[8,128]{1,0:T(8,128)} %bitcast.10, ...), custom_call_target="tpu_custom_call" | custom-call | tf_op jit(solution)/shard_map/solve/pallas_call | solution.py:585
  101.0 1.5 %copy.21 = bf16[64,512]{1,0:T(8,128)(2,1)} copy(bf16[64,512]{1,0:T(8,128)(2,1)} %get-tuple-element.4) | data formatting | bytes 131072
  102.4 1.5 %copy.22 = bf16[256,128]{1,0:T(8,128)(2,1)} copy(bf16[256,128]{1,0:T(8,128)(2,1)} %get-tuple-element.5) | data formatting | bytes 131072

commit v5 on v4

--- a/solution.py
+++ b/solution.py
@@ -12,7 +12,7 @@
 F32 = jnp.float32
 BF16 = jnp.bfloat16
 HIDE = -1e30
-LIFT = 16384.0
+LIFT = 2048.0
 LOG2E = 1.4426950408889634
 
 
@@ -100,10 +100,11 @@
         return copy
 
 
-def greet(devices):
+def greet(devices, meanwhile):
     barrier = pltpu.get_barrier_semaphore()
     for device in devices:
         pl.semaphore_signal(barrier, inc=1, device_id=device, device_id_type=MESH)
+    meanwhile()
     pl.semaphore_wait(barrier, len(devices))
 
 
@@ -151,26 +152,39 @@
         work(turn)
 
 
-def line_steps(zn):
-    return sorted([way * n for n in range(1, zn // 2 + 1) for way in (1, -1) if 2 * n < zn or way > 0], key=lambda n: -abs(n))
-
-
-def line_gather(sends, place, source, buffer, idle=()):
-    rows = source.shape[1]
-    found = {}
-    for step in line_steps(place.zn):
-        found[step] = first_hop(sends, place, source, buffer, step, False, (0, 1))
-    found[0] = first_hop(sends, place, source, buffer, 0, False, (1,))
-    first_hop(sends, place, source, buffer, 0, True, (0, 1))
+def direct_steps(zn):
+    if zn == 8:
+        return (2, -2, 1, -1)
+    return tuple(way * n for n in range(1, zn // 2 + 1) for way in (1, -1) if 2 * n < zn or way > 0)
+
+
+def stride_gather(sends, place, source, buffer, idle):
+    zn, rows = place.zn, source.shape[1]
+    steps = direct_steps(zn)
+    from_y = first_hop(sends, place, source, buffer, 0, True, (0, 1))
+    found = {(0, step): first_hop(sends, place, source, buffer, step, False, (0, 1)) for step in steps}
+    first_hop(sends, place, source, buffer, 0, False, (1,))
     buffer[aligned(place.c * rows, rows), :] = source[place.k]
-    for work in idle:
-        work()
-    for step in reversed(line_steps(place.zn)):
-        for copy in found[step]:
-            copy.receive()
-        chip = place.around(-step) * 2 + place.yl
-        piece = buffer.at[aligned(chip * 2 * rows, 2 * rows), :]
-        sends.make(piece, piece, place.device(0, True, False))
+    idle()
+
+    def piece(step, y):
+        return buffer.at[aligned((place.around(step) * 2 + y) * 2 * rows, 2 * rows), :]
+
+    for copy in from_y:
+        copy.receive()
+    theirs = piece(0, 1 - place.yl)
+    for step in steps:
+        found[1, step] = [sends.make(theirs, theirs, place.device(step, False, 0))]
+    if zn != 8:
+        return
+    for stream, y in ((0, place.yl), (1, 1 - place.yl)):
+        for way in (1, -1):
+            for copy in found[stream, 2 * way]:
+                copy.receive()
+            passed = piece(-2 * way, y)
+            sends.make(passed, passed, place.device(way, False, 0))
+            if (way == 1) == (stream == 0):
+                sends.make(passed, passed, place.device(2 * way, False, 0))
 
 
 def pack(ref, out, top, total):
@@ -249,7 +263,6 @@
         loads.start(a, b)
         for a, b in ((gain_hbm, gain_ref), (kgain_hbm, kgain), (dow_hbm, dow_ref))
     ]
-    greet(place.near(line_steps(zn)) + [{"head": d} for d in others])
     new, slice_width = hidden.shape
     heads = part.shape[1]
     dim = part.shape[3] - 16
@@ -261,23 +274,27 @@
     chip_first = chip * 2 * new
     scale = dim ** (-0.5) * LOG2E
 
-    q_load.wait()
-    flat = q_in[...].reshape(new, 2 * width)
-    q_half[0] = flat[:, :width]
-    q_half[1] = flat[:, width:]
     kept, swaps = [], []
 
+    def flatten():
+        q_load.wait()
+        flat = (q_in[...].reshape(new, 2 * width).astype(F32) * scale).astype(BF16)
+        q_half[0] = flat[:, :width]
+        q_half[1] = flat[:, width:]
+        for which in (0, 1):
+            for copy in kv_loads[which]:
+                copy.wait()
+            for value, count, at in ((old_in[which], cached, 0), (new_in[which], new, cached)):
+                flat = value.reshape(count, 2 * width)
+                rows = pl.ds(at, count)
+                kv_half[which, 0, rows, :] = flat[:, :width]
+                kv_half[which, 1, rows, :] = flat[:, width:]
+
+    greet(place.near(direct_steps(zn)) + [{"head": d} for d in others], flatten)
+
     def swap(which, out):
-        for copy in kv_loads[which]:
-            copy.wait()
-        for value, count, at, to in (
-            (old_in[which], cached, 0, k * cached),
-            (new_in[which], new, cached, 2 * cached + k * new),
-        ):
-            flat = value.reshape(count, 2 * width)
+        for count, at, to in ((cached, 0, k * cached), (new, cached, 2 * cached + k * new)):
             rows = pl.ds(at, count)
-            kv_half[which, 0, rows, :] = flat[:, :width]
-            kv_half[which, 1, rows, :] = flat[:, width:]
             target = out.at[aligned(to, count), :]
             swaps.append(sends.make(kv_half.at[which, 1 - k, rows, :], target, peer))
             kept.append(loads.start(kv_half.at[which, k, rows, :], target))
@@ -331,9 +348,9 @@
             scores.append(jnp.concatenate([found[: 2 * cached], late], axis=0))
         weights = []
         for found in scores:
-            top = jnp.max(found, axis=0, keepdims=True) * scale - LIFT * scale
+            top = jnp.max(found, axis=0, keepdims=True) - LIFT
             top = top.astype(BF16).astype(F32)
-            weights.append((top, jnp.exp2(found * scale - (top + LIFT * scale))))
+            weights.append((top, jnp.exp2(found - (top + LIFT))))
         for h, (top, found) in enumerate(weights):
             total = jnp.sum(found, axis=0, keepdims=True)
             out = lax.dot_general(
@@ -496,7 +513,7 @@
             first = jnp.where(owners.astype(F32) >= begins, begins, first)
         span[...] = first.astype(jnp.int32)
 
-    line_gather(sends, place, kv_tile, kvg, [byte_spans])
+    stride_gather(sends, place, kv_tile, kvg, byte_spans)
     for copy in sends.made:
         copy.receive()
     spans = (span, bp_both)
@@ -541,6 +558,12 @@
         own = own + bs_in[i].astype(F32)
     byte_out[...] = own.astype(BF16)
     sends.close()
+
+
+def hand_over(a, b, a_out, b_out, sem):
+    loads = Loads(sem)
+    for copy in (loads.start(a, a_out), loads.start(b, b_out)):
+        copy.wait()
 
 
 def per_device(
@@ -580,9 +603,9 @@
     half = dec_width // 2
     steps = max(zn // 2, 1)
     peers = max(hn - 1, 1)
-    copies = 5 + 7 + 4 * zn + 2 + 4 * (zn - 1) + 3 + 3 * (hn - 1) + 3 + 3 * (zn - 1) + 1
+    copies = 5 + 7 + 4 * zn + 2 + 4 * (zn - 1) + 3 + 3 * (hn - 1) + 3 + 4 * zn + 1
     flat_weight = out_weight.reshape(heads * dim, -1)
-    return pl.pallas_call(
+    results = pl.pallas_call(
         functools.partial(solve, zn, hn),
         out_shape=(
             jax.ShapeDtypeStruct(patch_hidden.shape, BF16),
@@ -659,6 +682,15 @@
         byte_patch.reshape(1, bytes_),
         mates,
     )
+    return pl.pallas_call(
+        hand_over,
+        out_shape=tuple(jax.ShapeDtypeStruct(r.shape, r.dtype) for r in results),
+        in_specs=[in_place()] * 2,
+        out_specs=(in_place(),) * 2,
+        scratch_shapes=[pltpu.SemaphoreType.DMA((2,))],
+        compiler_params=pltpu.CompilerParams(vmem_limit_bytes=60 * 2**20),
+        name="hand_over",
+    )(*results)
 
 
 def solution(mesh):

time: 104 us -> 102 us (0.981)
  local copies, waits for them, and re-layouts: 2.95 us -> 0 us
    pallas_call x0 -> x1, Pallas kernels: none -> 5.09 us  [per_device(): pl.pallas_call(hand_over, out_shape=tuple((jax.ShapeDtypeStruct(r.shape,...]
    pallas_call x1, Pallas kernels: 100 us -> 95.6 us  [per_device(): pl.pallas_call(functools.partial(solve, zn, hn), out_shape=(jax.ShapeDtyp...]
    unnamed x2 -> x0, local copies, waits for them, and re-layouts: 2.95 us -> none
where the time goes in v5:
time: 102 us; the launch traced here: 101 us
  Pallas kernels  101 us (99%)
    pallas_call x1, Pallas kernels, per_device(): pl.pallas_call(functools.partial(solve, zn, hn), out_shape=(jax.ShapeDtyp...  95.6 us
    pallas_call x1, Pallas kernels, per_device(): pl.pallas_call(hand_over, out_shape=tuple((jax.ShapeDtypeStruct(r.shape,...  5.09 us

profile of v5, /device:TPU:1, one launch (start us, length us, event | category | flops | bytes accessed | tf_op | source)
XLA Modules:
  0.0 101.5 jit_solution(7966231083065935413)
XLA Ops:
  0.6 95.6 %solve.1 = (bf16[64,512]{1,0:T(8,128)(2,1)}, bf16[256,128]{1,0:T(8,128)(2,1)}) custom-call(bf16[64,4,128]{2,1,0:T(4,128)(2,1)} %q_hbm.1, bf16[64,4,128]{2,1,0:T(4,128)(2,1)} %nk_hbm.1, bf16[64,4,128]{2,1,0:T(4,128)(2,1)} %nv_hbm.1, bf16[1024,4,128]{2,1,0:T(4,128)(2,1)} %ck_hbm.1, bf16[1024,4,128]{2,1,0:T(4,128)(2,1)} %cv_hbm.1, s32[8,128]{1,0:T(8,128)} %bitcast.10, ...), custom_call_target="tpu_custom_call" | custom-call | tf_op jit(solution)/shard_map/solve/pallas_call | solution.py:608
  96.2 5.1 %hand_over.1 = (bf16[64,512]{1,0:T(8,128)(2,1)}, bf16[256,128]{1,0:T(8,128)(2,1)}) custom-call(bf16[64,512]{1,0:T(8,128)(2,1)} %get-tuple-element.4.a, bf16[256,128]{1,0:T(8,128)(2,1)} %get-tuple-element.5.b), custom_call_target="tpu_custom_call" | custom-call | tf_op jit(solution)/shard_map/hand_over/pallas_call | solution.py:685

commit v6 on v5

--- a/solution.py
+++ b/solution.py
@@ -118,73 +118,54 @@
     return [sends.make(source.at[place.cores[core]], mine, place.device(step, other_y, core)) for core in cores]
 
 
-def ring_gather(sends, place, source, buffer, early, work):
-    zn = place.zn
-    rows = source.shape[1]
-    far, near = zn // 2, zn - 1 - zn // 2
-    arrived = {}
-    for way, count in ((1, far), (-1, near)):
-        if count:
-            for core, copy in enumerate(first_hop(sends, place, source, buffer, way, False, (0, 1))):
-                arrived[0, core, way, 0] = copy
-    from_y = first_hop(sends, place, source, buffer, 0, True, (0, 1))
-    from_core = first_hop(sends, place, source, buffer, 0, False, (1,))
-    buffer[aligned(place.c * rows, rows), :] = source[place.k]
-    early()
-    for turn in range(far + 1):
-        for stream, step in ((0, turn + 1), (1, turn)):
-            y = place.yl if stream == 0 else 1 - place.yl
-            counts = (far, near) if stream == 0 else (near, far)
-            for core in (0, 1):
-                for way, count in zip((1, -1), counts):
-                    if step >= count:
-                        continue
-                    (arrived[stream, core, way, step - 1] if step else from_y[core]).receive()
-                    owner = place.around(-way * step) * 4 + y * 2 + place.cores[core]
-                    piece = buffer.at[aligned(owner * rows, rows), :]
-                    arrived[stream, core, way, step] = sends.make(piece, piece, place.device(way, False, 0))
-        if turn == 0:
-            for copy in from_y + from_core:
-                copy.receive()
-        for (_, _, _, step), copy in list(arrived.items()):
-            if step == turn - 1:
-                copy.receive()
-        work(turn)
-
-
 def direct_steps(zn):
     if zn == 8:
         return (2, -2, 1, -1)
     return tuple(way * n for n in range(1, zn // 2 + 1) for way in (1, -1) if 2 * n < zn or way > 0)
 
 
-def stride_gather(sends, place, source, buffer, idle):
+def stride_gather(sends, place, source, buffer, idle, work):
     zn, rows = place.zn, source.shape[1]
+    far = zn // 2
+    arriving = [[] for _ in range(far + 1)]
+
+    def first(step, other_y, cores):
+        return first_hop(sends, place, source, buffer, step, other_y, cores)
+
+    def piece(step, y):
+        return buffer.at[aligned((place.around(step) * 2 + y) * 2 * rows, 2 * rows), :]
+
     steps = direct_steps(zn)
-    from_y = first_hop(sends, place, source, buffer, 0, True, (0, 1))
-    found = {(0, step): first_hop(sends, place, source, buffer, step, False, (0, 1)) for step in steps}
-    first_hop(sends, place, source, buffer, 0, False, (1,))
+    from_y = first(0, True, (0, 1))
+    found = {(0, step): first(step, False, (0, 1)) for step in steps}
+    arriving[0] += first(0, False, (1,))
     buffer[aligned(place.c * rows, rows), :] = source[place.k]
     idle()
-
-    def piece(step, y):
-        return buffer.at[aligned((place.around(step) * 2 + y) * 2 * rows, 2 * rows), :]
-
     for copy in from_y:
         copy.receive()
     theirs = piece(0, 1 - place.yl)
     for step in steps:
         found[1, step] = [sends.make(theirs, theirs, place.device(step, False, 0))]
-    if zn != 8:
-        return
-    for stream, y in ((0, place.yl), (1, 1 - place.yl)):
+    for (_, step), copies in found.items():
+        arriving[abs(step)] += copies
+
+    def relay(stream):
         for way in (1, -1):
             for copy in found[stream, 2 * way]:
                 copy.receive()
-            passed = piece(-2 * way, y)
-            sends.make(passed, passed, place.device(way, False, 0))
+            passed = piece(-2 * way, 1 - place.yl if stream else place.yl)
+            arriving[3].append(sends.make(passed, passed, place.device(way, False, 0)))
             if (way == 1) == (stream == 0):
-                sends.make(passed, passed, place.device(2 * way, False, 0))
+                arriving[4].append(sends.make(passed, passed, place.device(2 * way, False, 0)))
+
+    if zn == 8:
+        relay(0)
+    for n in range(far + 1):
+        if n == 1 and zn == 8:
+            relay(1)
+        for copy in arriving[n]:
+            copy.receive()
+        work(n)
 
 
 def pack(ref, out, top, total):
@@ -315,12 +296,12 @@
             copy.wait()
         held_swap = sends.make(held.at[k], held.at[k], peer)
         swap(0, kc)
-        swap(1, vc)
         cuts = [
             jnp.sum(jnp.where(nr[...] < r, 1.0, 0.0), axis=1, keepdims=True) for r in range(9)
         ]
         query_mark[...] = marks(positions(query_mark.shape[0], 0), cuts).astype(BF16)
         key_mark[2 * cached :, :] = (LIFT * marks(positions(2 * new, chip_first), cuts)).astype(BF16)
+        swap(1, vc)
         held_swap.receive()
         both = held[...]
         cuts = [
@@ -400,7 +381,7 @@
         if turn == far:
             reduce_step(0, (far,))
 
-    ring_gather(sends, place, q_half, qg, early, work)
+    stride_gather(sends, place, q_half, qg, early, work)
 
     swapped = []
 
@@ -513,7 +494,7 @@
             first = jnp.where(owners.astype(F32) >= begins, begins, first)
         span[...] = first.astype(jnp.int32)
 
-    stride_gather(sends, place, kv_tile, kvg, byte_spans)
+    stride_gather(sends, place, kv_tile, kvg, byte_spans, lambda n: None)
     for copy in sends.made:
         copy.receive()
     spans = (span, bp_both)
@@ -560,9 +541,11 @@
     sends.close()
 
 
-def hand_over(a, b, a_out, b_out, sem):
+def hand_over(a, b, a_out, b_out, a_held, b_held, sem):
     loads = Loads(sem)
-    for copy in (loads.start(a, a_out), loads.start(b, b_out)):
+    for copy in (loads.start(a, a_held), loads.start(b, b_held)):
+        copy.wait()
+    for copy in (loads.start(a_held, a_out), loads.start(b_held, b_out)):
         copy.wait()
 
 
@@ -687,7 +670,7 @@
         out_shape=tuple(jax.ShapeDtypeStruct(r.shape, r.dtype) for r in results),
         in_specs=[in_place()] * 2,
         out_specs=(in_place(),) * 2,
-        scratch_shapes=[pltpu.SemaphoreType.DMA((2,))],
+        scratch_shapes=[VMEM(r.shape, r.dtype) for r in results] + [pltpu.SemaphoreType.DMA((4,))],
         compiler_params=pltpu.CompilerParams(vmem_limit_bytes=60 * 2**20),
         name="hand_over",
     )(*results)

time: 102 us -> 99.7 us (0.977)
  Pallas kernels: 101 us -> 98.8 us
    pallas_call x1, Pallas kernels: 5.09 us -> 1.56 us  [per_device(): pl.pallas_call(hand_over, out_shape=tuple((jax.ShapeDtypeStruct(r.shape,...]
    pallas_call x1, Pallas kernels: 95.6 us -> 97.2 us  [per_device(): pl.pallas_call(functools.partial(solve, zn, hn), out_shape=(jax.ShapeDtyp...]
where the time goes in v6:
time: 99.7 us; the launch traced here: 99.6 us
  Pallas kernels  98.8 us (99%)
    pallas_call x1, Pallas kernels, per_device(): pl.pallas_call(functools.partial(solve, zn, hn), out_shape=(jax.ShapeDtyp...  97.2 us

profile of v6, /device:TPU:1, one launch (start us, length us, event | category | flops | bytes accessed | tf_op | source)
XLA Modules:
  0.0 99.6 jit_solution(2016630440539330610)
XLA Ops:
  0.6 97.2 %solve.1 = (bf16[64,512]{1,0:T(8,128)(2,1)}, bf16[256,128]{1,0:T(8,128)(2,1)}) custom-call(bf16[64,4,128]{2,1,0:T(4,128)(2,1)} %q_hbm.1, bf16[64,4,128]{2,1,0:T(4,128)(2,1)} %nk_hbm.1, bf16[64,4,128]{2,1,0:T(4,128)(2,1)} %nv_hbm.1, bf16[1024,4,128]{2,1,0:T(4,128)(2,1)} %ck_hbm.1, bf16[1024,4,128]{2,1,0:T(4,128)(2,1)} %cv_hbm.1, s32[8,128]{1,0:T(8,128)} %bitcast.10, ...), custom_call_target="tpu_custom_call" | custom-call | tf_op jit(solution)/shard_map/solve/pallas_call | solution.py:591
  97.9 1.6 %hand_over.1 = (bf16[64,512]{1,0:T(8,128)(2,1)}, bf16[256,128]{1,0:T(8,128)(2,1)}) custom-call(bf16[64,512]{1,0:T(8,128)(2,1)} %get-tuple-element.4.a, bf16[256,128]{1,0:T(8,128)(2,1)} %get-tuple-element.5.b), custom_call_target="tpu_custom_call" | custom-call | tf_op jit(solution)/shard_map/hand_over/pallas_call | solution.py:668

commit v7 on v6

--- a/solution.py
+++ b/solution.py
@@ -44,7 +44,7 @@
     def near(self, steps):
         found = [self.device(0, False, True)]
         for core in (False, True):
-            found.append(self.device(0, True, core))
+            found += [self.device(step, True, core) for step in (0, 1, -1)]
             found += [self.device(step, False, core) for step in steps]
         return found
 
@@ -163,6 +163,48 @@
     for n in range(far + 1):
         if n == 1 and zn == 8:
             relay(1)
+        for copy in arriving[n]:
+            copy.receive()
+        work(n)
+
+
+def cross_gather(sends, place, source, buffer, idle, work):
+    rows = source.shape[1]
+    arriving = [[] for _ in range(5)]
+
+    def first(step, other_y, cores=(0, 1)):
+        return first_hop(sends, place, source, buffer, step, other_y, cores)
+
+    def piece(step):
+        return buffer.at[aligned((place.around(step) * 2 + place.yl) * 2 * rows, 2 * rows), :]
+
+    def across(step):
+        passed = piece(step)
+        return sends.make(passed, passed, place.device(0, True, False))
+
+    found = {step: first(step, False) for step in (2, -2)}
+    arriving[0] += first(0, True) + first(0, False, (1,))
+    for step in (1, -1):
+        arriving[1] += first(step, False) + first(step, True)
+    buffer[aligned(place.c * rows, rows), :] = source[place.k]
+    idle()
+    relayed = {}
+    for way in (1, -1):
+        for copy in found[2 * way]:
+            copy.receive()
+        passed = piece(-2 * way)
+        relayed[way] = sends.make(passed, passed, place.device(way, False, 0))
+    side = 1 - 2 * place.k
+    passed = piece(-2 * side)
+    opposite = sends.make(passed, passed, place.device(2 * side, False, 0))
+    arriving[2] += [across(-2), across(2)]
+    for n in range(5):
+        if n == 2:
+            for way in (1, -1):
+                relayed[way].receive()
+                arriving[3].append(across(-3 * way))
+            opposite.receive()
+            arriving[4].append(across(4))
         for copy in arriving[n]:
             copy.receive()
         work(n)
@@ -381,7 +423,8 @@
         if turn == far:
             reduce_step(0, (far,))
 
-    stride_gather(sends, place, q_half, qg, early, work)
+    gather = cross_gather if zn == 8 else stride_gather
+    gather(sends, place, q_half, qg, early, work)
 
     swapped = []
 

time: 99.7 us -> 98.3 us (0.986)
  Pallas kernels: 98.8 us -> 97.3 us
    pallas_call x1, Pallas kernels: 97.2 us -> 95.8 us  [per_device(): pl.pallas_call(functools.partial(solve, zn, hn), out_shape=(jax.ShapeDtyp...]
where the time goes in v7:
time: 98.3 us; the launch traced here: 98.1 us
  Pallas kernels  97.3 us (99%)
    pallas_call x1, Pallas kernels, per_device(): pl.pallas_call(functools.partial(solve, zn, hn), out_shape=(jax.ShapeDtyp...  95.8 us

profile of v7, /device:TPU:1, one launch (start us, length us, event | category | flops | bytes accessed | tf_op | source)
XLA Modules:
  0.0 98.1 jit_solution(10985419524701108190)
XLA Ops:
  0.6 95.8 %solve.1 = (bf16[64,512]{1,0:T(8,128)(2,1)}, bf16[256,128]{1,0:T(8,128)(2,1)}) custom-call(bf16[64,4,128]{2,1,0:T(4,128)(2,1)} %q_hbm.1, bf16[64,4,128]{2,1,0:T(4,128)(2,1)} %nk_hbm.1, bf16[64,4,128]{2,1,0:T(4,128)(2,1)} %nv_hbm.1, bf16[1024,4,128]{2,1,0:T(4,128)(2,1)} %ck_hbm.1, bf16[1024,4,128]{2,1,0:T(4,128)(2,1)} %cv_hbm.1, s32[8,128]{1,0:T(8,128)} %bitcast.10, ...), custom_call_target="tpu_custom_call" | custom-call | tf_op jit(solution)/shard_map/solve/pallas_call | solution.py:634
  96.4 1.6 %hand_over.1 = (bf16[64,512]{1,0:T(8,128)(2,1)}, bf16[256,128]{1,0:T(8,128)(2,1)}) custom-call(bf16[64,512]{1,0:T(8,128)(2,1)} %get-tuple-element.4.a, bf16[256,128]{1,0:T(8,128)(2,1)} %get-tuple-element.5.b), custom_call_target="tpu_custom_call" | custom-call | tf_op jit(solution)/shard_map/hand_over/pallas_call | solution.py:711

commit v8 on v7

--- a/solution.py
+++ b/solution.py
@@ -276,16 +276,7 @@
         (loads.start(cv_hbm, old_in.at[1]), loads.start(nv_hbm, new_in.at[1])),
     ]
     small = [loads.start(cr_hbm, held.at[k]), loads.start(nr_hbm, nr)]
-    for_queries = [
-        loads.start(a, b)
-        for a, b in ((states_hbm, states_ref), (dqw_hbm, dqw_ref), (qgain_hbm, qgain), (bp_hbm, bp_both.at[k]))
-    ]
-    dkv_load = loads.start(dkv_hbm, dkv_in)
-    w_loads = [loads.start(w_hbm, w_ref), loads.start(hidden_hbm, hidden)]
-    late = [
-        loads.start(a, b)
-        for a, b in ((gain_hbm, gain_ref), (kgain_hbm, kgain), (dow_hbm, dow_ref))
-    ]
+    for_queries, dkv_loads, w_loads, late = [], [], [], []
     new, slice_width = hidden.shape
     heads = part.shape[1]
     dim = part.shape[3] - 16
@@ -333,11 +324,21 @@
     def positions(count, first):
         return (lax.broadcasted_iota(jnp.int32, (count, query_mark.shape[1]), 0) + first).astype(F32)
 
+    def later_loads():
+        for group, pairs in (
+            (for_queries, ((states_hbm, states_ref), (dqw_hbm, dqw_ref), (qgain_hbm, qgain), (bp_hbm, bp_both.at[k]))),
+            (dkv_loads, ((dkv_hbm, dkv_in),)),
+            (w_loads, ((w_hbm, w_ref), (hidden_hbm, hidden))),
+            (late, ((gain_hbm, gain_ref), (kgain_hbm, kgain), (dow_hbm, dow_ref))),
+        ):
+            group += [loads.start(a, b) for a, b in pairs]
+
     def early():
         for copy in small:
             copy.wait()
         held_swap = sends.make(held.at[k], held.at[k], peer)
         swap(0, kc)
+        later_loads()
         cuts = [
             jnp.sum(jnp.where(nr[...] < r, 1.0, 0.0), axis=1, keepdims=True) for r in range(9)
         ]
@@ -443,7 +444,7 @@
         bq[rows, :] = bq_tile[k]
 
     def flat_weights():
-        dkv_load.wait()
+        dkv_loads[0].wait()
         count = dkv.shape[0] // 4
         for i in range(4):
             rows = slice(i * count, (i + 1) * count)

time: 98.3 us -> 98.3 us (level)
  no operation moved by 1% of the time
where the time goes in v8:
time: 98.3 us; the launch traced here: 98.1 us
  Pallas kernels  97.3 us (99%)
    pallas_call x1, Pallas kernels, per_device(): pl.pallas_call(functools.partial(solve, zn, hn), out_shape=(jax.ShapeDtyp...  95.7 us

profile of v8, /device:TPU:1, one launch (start us, length us, event | category | flops | bytes accessed | tf_op | source)
XLA Modules:
  0.0 98.1 jit_solution(1804162602216308939)
XLA Ops:
  0.6 95.7 %solve.1 = (bf16[64,512]{1,0:T(8,128)(2,1)}, bf16[256,128]{1,0:T(8,128)(2,1)}) custom-call(bf16[64,4,128]{2,1,0:T(4,128)(2,1)} %q_hbm.1, bf16[64,4,128]{2,1,0:T(4,128)(2,1)} %nk_hbm.1, bf16[64,4,128]{2,1,0:T(4,128)(2,1)} %nv_hbm.1, bf16[1024,4,128]{2,1,0:T(4,128)(2,1)} %ck_hbm.1, bf16[1024,4,128]{2,1,0:T(4,128)(2,1)} %cv_hbm.1, s32[8,128]{1,0:T(8,128)} %bitcast.10, ...), custom_call_target="tpu_custom_call" | custom-call | tf_op jit(solution)/shard_map/solve/pallas_call | solution.py:635
  96.4 1.6 %hand_over.1 = (bf16[64,512]{1,0:T(8,128)(2,1)}, bf16[256,128]{1,0:T(8,128)(2,1)}) custom-call(bf16[64,512]{1,0:T(8,128)(2,1)} %get-tuple-element.4.a, bf16[256,128]{1,0:T(8,128)(2,1)} %get-tuple-element.5.b), custom_call_target="tpu_custom_call" | custom-call | tf_op jit(solution)/shard_map/hand_over/pallas_call | solution.py:712
